TPU v7x, 256 devices: a whole 4x4x8 slice. The times are simulated.
256 devices in a mesh: section: 64 (over z, y, core), tensor: 4 (over x).
Axes of the slice: x: 4, y: 4, z: 8, core: 2. Of those that a mesh axis runs over, the one named last changes fastest.
Arguments:
- inner_input: bfloat16 [2, 2048, 8192], P(None, 'section', 'tensor'), may hold values from -6 to 6
- gate_input: bfloat16 [2, 2048, 8192], P(None, 'section', 'tensor'), may hold values from -6 to 6
- conv_state: bfloat16 [2048, 3, 8192], P('section', None, 'tensor'), may hold values from -6 to 6
- mamba_state: bfloat16 [2048, 16, 8192], P('section', None, 'tensor'), may hold values from -6 to 6
- conv_weight: float32 [4, 8192], P(None, 'tensor'), may hold values from -3 to 3
- conv_bias: float32 [8192], P('tensor'), may hold values from -0.5 to 0.5
- xproj_weight: bfloat16 [544, 8192], P(None, 'tensor'), may hold values from -0.0625 to 0.0625
- dt_gain: float32 [512], replicated, may hold values from 0.5 to 1.5
- dtproj_weight: bfloat16 [512, 8192], P(None, 'tensor'), may hold values from -0.25 to 0.25
- dt_bias: float32 [8192], P('tensor'), may hold values from -4 to -1
- decay_rate: float32 [16, 8192], P(None, 'tensor'), may hold values from 0.05 to 2
- skip_gain: float32 [8192], P('tensor'), may hold values from 0.5 to 1.5
- query: bfloat16 [2, 2048, 8192], P(None, 'section', 'tensor'), may hold values from -14 to 14
- key_cache: bfloat16 [2048, 32, 1024], P('section', None, 'tensor'), may hold values from -6 to 6
- value_cache: bfloat16 [2048, 32, 1024], P('section', None, 'tensor'), may hold values from -6 to 6
- key_new: bfloat16 [2, 2048, 1024], P(None, 'section', 'tensor'), may hold values from -6 to 6
- value_new: bfloat16 [2, 2048, 1024], P(None, 'section', 'tensor'), may hold values from -6 to 6
- kv_length: int32 [2048], P('section'), may hold values from 2 to 30, as said below
- new_owner: int32 [2048], replicated, may hold values from 0 to 63, as said below
Outputs:
- mamba_out: bfloat16 [2, 2048, 8192], P(None, 'section', 'tensor')
- attn_out: bfloat16 [2, 2048, 8192], P(None, 'section', 'tensor')
- moved_conv: bfloat16 [2048, 3, 8192], P('section', None, 'tensor')
- moved_state: bfloat16 [2048, 16, 8192], P('section', None, 'tensor')
- moved_keys: bfloat16 [2048, 32, 1024], P('section', None, 'tensor')
- moved_values: bfloat16 [2048, 32, 1024], P('section', None, 'tensor')
Inputs may be any that keep to these rules, and one draw needn't show every extreme that they name: `new_owner`: for every local slot number j, each section index receives exactly one request that stands in slot j of some section index, and it takes slot j; one section index sends at most 1 request to one section index, and some pairs reach 1. `kv_length`: some request has each bound.
All inputs are finite; a program needn't handle non-finite values.
Results may differ from a plain program's by a relative error of at most 0.0052.
Values may be sent and summed in bfloat16 or wider, within the bound.
A program may use at most 128 MiB of HBM per device.

v0:
```python
import math

import jax
import jax.numpy as jnp
from jax import lax
from jax.sharding import PartitionSpec as P

HEAD = 128


epsilon = 1e-06


def project_rows(conv_rows, xproj_weight):
    return lax.dot_general(
        conv_rows, xproj_weight, (((1,), (1,)), ((), ())), preferred_element_type=jnp.float32
    )


def slot_ranks(owners):
    slot_count = owners.shape[-1]
    slot_order = jnp.arange(slot_count, dtype=jnp.int32)
    earlier = slot_order[None, :] < slot_order[:, None]
    matching = owners[..., :, None] == owners[..., None, :]
    return jnp.sum(jnp.where(matching & earlier, 1, 0), axis=-1).astype(jnp.int32)


def pack_slots(values_in, send_slots, total_slots):
    return (
        jnp.zeros((total_slots,) + values_in.shape[1:], values_in.dtype)
        .at[send_slots]
        .set(values_in)
    )


def local(
    inner_input,
    gate_input,
    conv_state,
    mamba_state,
    conv_weight,
    conv_bias,
    xproj_weight,
    dt_gain,
    dtproj_weight,
    dt_bias,
    decay_rate,
    skip_gain,
    query,
    key_cache,
    value_cache,
    key_new,
    value_new,
    kv_length,
    new_owner,
):
    steps_count = inner_input.shape[0]
    requests_here = inner_input.shape[1]
    channels = inner_input.shape[2]
    tap_count = conv_weight.shape[0]
    rank_width = dt_gain.shape[0]
    state_width = mamba_state.shape[1]
    sections = lax.axis_size("section")
    section_index = lax.axis_index("section")
    capacity = max(1, requests_here // sections)
    total_slots = sections * capacity
    owners = new_owner.reshape(sections, requests_here)
    my_owners = lax.dynamic_slice_in_dim(owners, section_index, 1, 0)[0]
    send_slots = my_owners * capacity + slot_ranks(my_owners)
    ranks_all = slot_ranks(owners)
    arriving = owners == section_index
    sources = jnp.arange(sections, dtype=jnp.int32)[:, None]
    recv_slots = jnp.sum(jnp.where(arriving, sources * capacity + ranks_all, 0), axis=0)
    window = jnp.concatenate([conv_state, jnp.swapaxes(inner_input, 0, 1)], axis=1)
    conv_list = []
    for step_index in range(steps_count):
        summed = jnp.zeros((requests_here, channels), jnp.float32) + conv_bias
        for tap_index in range(tap_count):
            summed = summed + conv_weight[tap_index] * window[:, step_index + tap_index].astype(
                jnp.float32
            )
        conv_list.append(jax.nn.silu(summed).astype(jnp.bfloat16))
    conv_out = jnp.stack(conv_list)
    hidden = mamba_state.astype(jnp.float32)
    mamba_list = []
    for step_index in range(steps_count):
        projected = lax.psum(project_rows(conv_out[step_index], xproj_weight), "tensor")
        low_rank = projected[:, :rank_width]
        scaled = (
            low_rank
            * lax.rsqrt(jnp.mean(low_rank * low_rank, axis=-1, keepdims=True) + epsilon)
            * dt_gain
        ).astype(jnp.bfloat16)
        delta_rate = jax.nn.softplus(
            jnp.dot(scaled, dtproj_weight, preferred_element_type=jnp.float32) + dt_bias
        )
        input_gain = projected[:, rank_width : rank_width + state_width]
        output_gain = projected[:, rank_width + state_width :]
        inputs_now = conv_out[step_index].astype(jnp.float32)
        hidden = (
            jnp.exp(-delta_rate[:, None, :] * decay_rate[None]) * hidden
            + (delta_rate * inputs_now)[:, None, :] * input_gain[:, :, None]
        )
        reading = jnp.sum(hidden * output_gain[:, :, None], axis=1) + skip_gain * inputs_now
        mamba_list.append(
            (reading * jax.nn.silu(gate_input[step_index].astype(jnp.float32))).astype(jnp.bfloat16)
        )
    final_state = hidden.astype(jnp.bfloat16)
    final_conv = window[:, steps_count:]
    cache_slots = key_cache.shape[1]
    cache_heads = key_cache.shape[2] // HEAD
    query_heads = query.shape[2] // HEAD
    group_size = query_heads // cache_heads
    positions = jnp.arange(cache_slots, dtype=jnp.int32)
    key_rows = key_cache
    value_rows = value_cache
    attended = []
    for step_index in range(steps_count):
        target = kv_length + step_index
        written = (positions[None, :] == target[:, None])[:, :, None]
        key_rows = jnp.where(written, key_new[step_index][:, None, :], key_rows)
        value_rows = jnp.where(written, value_new[step_index][:, None, :], value_rows)
        queries = query[step_index].reshape(requests_here, cache_heads, group_size, HEAD)
        key_heads = key_rows.reshape(requests_here, cache_slots, cache_heads, HEAD)
        scores = jnp.einsum(
            "rgqd,rcgd->rgqc", queries, key_heads, preferred_element_type=jnp.float32
        ) / math.sqrt(HEAD)
        allowed = (positions[None, :] <= target[:, None])[:, None, None, :]
        scores = jnp.where(allowed, scores, -1e30)
        highest = jnp.max(scores, axis=-1, keepdims=True)
        weights = jnp.exp(scores - highest)
        weights = (weights / jnp.sum(weights, axis=-1, keepdims=True)).astype(jnp.bfloat16)
        value_heads = value_rows.reshape(requests_here, cache_slots, cache_heads, HEAD)
        mixed_out = jnp.einsum(
            "rgqc,rcgd->rgqd", weights, value_heads, preferred_element_type=jnp.float32
        )
        attended.append(mixed_out.reshape(requests_here, query_heads * HEAD).astype(jnp.bfloat16))
    moved_conv, moved_state, moved_keys, moved_values = (
        lax.all_to_all(
            pack_slots(final_conv, send_slots, total_slots),
            "section",
            split_axis=0,
            concat_axis=0,
            tiled=True,
        ),
        lax.all_to_all(
            pack_slots(final_state, send_slots, total_slots),
            "section",
            split_axis=0,
            concat_axis=0,
            tiled=True,
        ),
        lax.all_to_all(
            pack_slots(key_rows, send_slots, total_slots),
            "section",
            split_axis=0,
            concat_axis=0,
            tiled=True,
        ),
        lax.all_to_all(
            pack_slots(value_rows, send_slots, total_slots),
            "section",
            split_axis=0,
            concat_axis=0,
            tiled=True,
        ),
    )
    return (
        jnp.stack(mamba_list),
        jnp.stack(attended),
        jnp.take(moved_conv, recv_slots, axis=0),
        jnp.take(moved_state, recv_slots, axis=0),
        jnp.take(moved_keys, recv_slots, axis=0),
        jnp.take(moved_values, recv_slots, axis=0),
    )


def solution(mesh):
    in_specs = (
        P(None, "section", "tensor"),
        P(None, "section", "tensor"),
        P("section", None, "tensor"),
        P("section", None, "tensor"),
        P(None, "tensor"),
        P("tensor"),
        P(None, "tensor"),
        P(),
        P(None, "tensor"),
        P("tensor"),
        P(None, "tensor"),
        P("tensor"),
        P(None, "section", "tensor"),
        P("section", None, "tensor"),
        P("section", None, "tensor"),
        P(None, "section", "tensor"),
        P(None, "section", "tensor"),
        P("section"),
        P(),
    )
    out_specs = (
        P(None, "section", "tensor"),
        P(None, "section", "tensor"),
        P("section", None, "tensor"),
        P("section", None, "tensor"),
        P("section", None, "tensor"),
        P("section", None, "tensor"),
    )
    return jax.shard_map(local, mesh=mesh, in_specs=in_specs, out_specs=out_specs, check_vma=False)
```

profile of v0, /device:TPU:1, one launch (start us, length us, event | category | flops | bytes accessed | tf_op | source)
XLA Modules:
  0.0 254.8 jit_solution(11777203651297937950)
XLA Ops:
  10.1 1.5 broadcast_in_dim.186
  11.6 4.4 %scatter_fusion = bf16[64,3,2048]{2,1,0:T(4,128)(2,1)} fusion(bf16[64,3,2048]{2,1,0:T(4,128)(2,1)} %broadcast_in_dim.186, s32[32]{0:T(128)S(1)} %fusion.69, bf16[32,3,2048]{2,1,0:T(4,128)(2,1)S(1)} %copy.42), kind=kCustom, calls=%fused_computation.4 | custom fusion | bytes 1179776 | tf_op jit(solution)/shard_map/scatter | solution.py:32
  16.0 13.3 %all-to-all-start = ((bf16[64,3,2048]{2,1,0:T(4,128)(2,1)}), bf16[64,3,2048]{2,1,0:T(4,128)(2,1)}, u32[]{:S(2)}, u32[]{:S(2)}) async-start(bf16[64,3,2048]{2,1,0:T(4,128)(2,1)} %scatter_fusion), calls=%async_computation | async-start | bytes 2097152 | tf_op jit(solution)/shard_map/all_to_all | solution.py:139
  30.0 2.4 fusion.20
  33.6 4.8 %scatter_fusion.2 = bf16[64,32,256]{2,1,0:T(8,128)(2,1)} fusion(bf16[64,32,256]{2,1,0:T(8,128)(2,1)} %broadcast.438.clone.1, s32[32]{0:T(128)S(1)} %fusion.69, bf16[32,32,256]{2,1,0:T(8,128)(2,1)} %get-tuple-element.50), kind=kCustom, calls=%fused_computation.6 | custom fusion | bytes 1572992 | tf_op jit(solution)/shard_map/scatter | solution.py:32
  38.4 18.8 %all-to-all-done = bf16[64,3,2048]{2,1,0:T(4,128)(2,1)} async-done(((bf16[64,3,2048]{2,1,0:T(4,128)(2,1)}), bf16[64,3,2048]{2,1,0:T(4,128)(2,1)}, u32[]{:S(2)}, u32[]{:S(2)}) %all-to-all-start) | async-done | bytes 786464 | tf_op jit(solution)/shard_map/all_to_all | solution.py:139
  57.2 6.7 %all-to-all-start.2 = ((bf16[64,32,256]{2,1,0:T(8,128)(2,1)}), bf16[64,32,256]{2,1,0:T(8,128)(2,1)}, u32[]{:S(2)}, u32[]{:S(2)}) async-start(bf16[64,32,256]{2,1,0:T(8,128)(2,1)} %scatter_fusion.2), calls=%async_computation.2 | async-start | bytes 2097152 | tf_op jit(solution)/shard_map/all_to_all | solution.py:153
  64.9 1.4 fusion.79
  66.3 1.4 fusion.80
  68.9 4.3 %scatter_fusion.3 = bf16[64,32,256]{2,1,0:T(8,128)(2,1)} fusion(bf16[64,32,256]{2,1,0:T(8,128)(2,1)} %broadcast.438.clone, s32[32]{0:T(128)S(1)} %fusion.69, bf16[32,32,256]{2,1,0:T(8,128)(2,1)S(1)} %get-tuple-element.31), kind=kCustom, calls=%fused_computation.7 | custom fusion | bytes 1572992 | tf_op jit(solution)/shard_map/scatter | solution.py:32
  73.2 18.5 %all-to-all-done.2 = bf16[64,32,256]{2,1,0:T(8,128)(2,1)} async-done(((bf16[64,32,256]{2,1,0:T(8,128)(2,1)}), bf16[64,32,256]{2,1,0:T(8,128)(2,1)}, u32[]{:S(2)}, u32[]{:S(2)}) %all-to-all-start.2) | async-done | bytes 1048608 | tf_op jit(solution)/shard_map/all_to_all | solution.py:153
  91.8 6.7 %all-to-all-start.3 = ((bf16[64,32,256]{2,1,0:T(8,128)(2,1)}), bf16[64,32,256]{2,1,0:T(8,128)(2,1)}, u32[]{:S(2)}, u32[]{:S(2)}) async-start(bf16[64,32,256]{2,1,0:T(8,128)(2,1)} %scatter_fusion.3), calls=%async_computation.3 | async-start | bytes 2097152 | tf_op jit(solution)/shard_map/all_to_all | solution.py:160
  98.4 15.7 %all-reduce.3.cloned.1.call-done = (f32[32,544]{1,0:T(8,128)}, f32[32,544]{1,0:T(8,128)}) async-done(((f32[32,544]{1,0:T(8,128)}, f32[32,544]{1,0:T(8,128)}), (f32[32,544]{1,0:T(8,128)}, f32[32,544]{1,0:T(8,128)})) %all-reduce.3.cloned.1.call-update) | async-done | bytes 139280 | tf_op jit(solution)/shard_map/psum | solution.py:87
  116.2 2.3 fusion.72
  119.2 6.0 %multiply_reduce_fusion.1 = (f32[32,2048]{1,0:T(8,128)}, f32[32,2048]{1,0:T(8,128)}, bf16[32,16,2048]{2,1,0:T(8,128)(2,1)}) fusion(bf16[32,16,2048]{2,1,0:T(8,128)(2,1)S(1)} %copy-done.4, f32[32,16]{1,0:T(8,128)S(1)} %get-tuple-element.60, f32[32,16]{1,0:T(8,128)S(1)} %get-tuple-element.61, f32[32,2048]{1,0:T(8,128)S(1)} %get-tuple-element.37, ...), kind=kLoop, calls=%fused_computation.12 | loop fusion | flops 14548992 | bytes 5906432 | tf_op jit(solution)/shard_map/reduce_sum | solution.py:104
  125.2 2.5 broadcast_in_dim.191
  127.6 6.2 %scatter_fusion.1 = bf16[64,16,2048]{2,1,0:T(8,128)(2,1)} fusion(bf16[64,16,2048]{2,1,0:T(8,128)(2,1)} %broadcast_in_dim.191, s32[32]{0:T(128)S(1)} %fusion.69, bf16[32,16,2048]{2,1,0:T(8,128)(2,1)} %get-tuple-element.23), kind=kCustom, calls=%fused_computation.5 | custom fusion | bytes 6291584 | tf_op jit(solution)/shard_map/scatter | solution.py:32
  133.9 12.3 %all-to-all-start.1 = ((bf16[64,16,2048]{2,1,0:T(8,128)(2,1)}), bf16[64,16,2048]{2,1,0:T(8,128)(2,1)}, u32[]{:S(2)}, u32[]{:S(2)}) async-start(bf16[64,16,2048]{2,1,0:T(8,128)(2,1)} %scatter_fusion.1), calls=%async_computation.1 | async-start | bytes 8388608 | tf_op jit(solution)/shard_map/all_to_all | solution.py:146
  146.3 1.7 slice_bitcast_fusion.1
  147.9 1.4 fusion.8
  150.3 2.7 %convolution_convert_fusion = bf16[32,2,8,128]{3,2,1,0:T(8,128)(2,1)} fusion(f32[32,2,8]{2,1,0:T(2,128)S(1)} %fusion.77, f32[32,2,8,32]{3,2,1,0:T(8,128)} %copy-done.10, bf16[32,32,256]{2,1,0:T(8,128)(2,1)S(1)} %get-tuple-element.31), kind=kOutput, calls=%fused_computation.28 | convolution fusion | flops 4309535 | bytes 722944 | tf_op jit(solution)/shard_map/rgqc,rcgd->rgqd/dot_general | solution.py:134
  154.9 1.5 fusion.6
  158.0 2.9 %convolution_convert_fusion.1 = bf16[32,2,8,128]{3,2,1,0:T(8,128)(2,1)} fusion(bf16[32,4,2,8,128]{4,3,2,1,0:T(8,128)(2,1)} %get-tuple-element.30, f32[32,2,8]{2,1,0:T(2,128)} %fusion.78, f32[32,2,8,32]{3,2,1,0:T(8,128)} %copy-done.9), kind=kOutput, calls=%fused_computation.29 | convolution fusion | flops 4309535 | bytes 722944 | tf_op jit(solution)/shard_map/rgqc,rcgd->rgqd/dot_general | solution.py:134
  160.9 1.6 convert_element_type.250
  162.9 1.6 pad_maximum_fusion.2
  164.6 1.4 fusion.62
  166.8 2.2 gather_fusion
  170.3 1.8 gather_fusion.2
  172.1 1.8 gather_fusion.3
  175.1 65.5 %all-to-all-done.1 = bf16[64,16,2048]{2,1,0:T(8,128)(2,1)} async-done(((bf16[64,16,2048]{2,1,0:T(8,128)(2,1)}), bf16[64,16,2048]{2,1,0:T(8,128)(2,1)}, u32[]{:S(2)}, u32[]{:S(2)}) %all-to-all-start.1) | async-done | bytes 4194336 | tf_op jit(solution)/shard_map/all_to_all | solution.py:146
  240.6 4.2 %gather_fusion.1 = bf16[32,16,2048]{2,1,0:T(8,128)(2,1)} fusion(bf16[64,16,2048]{2,1,0:T(8,128)(2,1)} %all-to-all-done.1, s32[1024]{0:T(1024)S(1)} %pad_clamp_fusion.1), kind=kCustom, calls=%fused_computation.3 | custom fusion | bytes 4194432 | tf_op jit(solution)/shard_map/jit(_take)/gather | solution.py:172
  244.8 3.2 %broadcast_select_fusion = bf16[32,16,2048]{2,1,0:T(8,128)(2,1)} fusion(bf16[32,16,2048]{2,1,0:T(8,128)(2,1)} %gather_fusion.1, pred[32]{0:T(512)(128)(4,1)S(1)} %compare_and_fusion), kind=kLoop, calls=%fused_computation.17 | loop fusion | flops 1048576 | bytes 4194336 | tf_op jit(solution)/shard_map/jit(_take)/select_n | solution.py:172
  (89 shorter events, 17.6 us)
Async XLA Ops:
  7.2 57.7 %copy-start = (bf16[544,2048]{1,0:T(8,128)(2,1)S(1)}, bf16[544,2048]{1,0:T(8,128)(2,1)}, u32[]{:S(2)}) copy-start(bf16[544,2048]{1,0:T(8,128)(2,1)} %param.27) | copy-start | bytes 6684676
  8.1 0.6 copy-start.11
  10.1 19.2 %copy-start.24 = (s32[32]{0:T(128)S(1)}, s32[32]{0:T(128)}, u32[]{:S(2)}) copy-start(s32[32]{0:T(128)} %param.38) | copy-start | bytes 388
  10.1 19.9 %copy-start.21 = (bf16[2,32,256]{2,1,0:T(8,128)(2,1)S(1)}, bf16[2,32,256]{2,1,0:T(8,128)(2,1)}, u32[]{:S(2)}) copy-start(bf16[2,32,256]{2,1,0:T(8,128)(2,1)} %param.37) | copy-start | bytes 98308
  10.1 19.9 %copy-start.22 = (bf16[2,32,256]{2,1,0:T(8,128)(2,1)S(1)}, bf16[2,32,256]{2,1,0:T(8,128)(2,1)}, u32[]{:S(2)}) copy-start(bf16[2,32,256]{2,1,0:T(8,128)(2,1)} %param.36) | copy-start | bytes 98308
  16.0 41.3 %all-to-all-start = ((bf16[64,3,2048]{2,1,0:T(4,128)(2,1)}), bf16[64,3,2048]{2,1,0:T(4,128)(2,1)}, u32[]{:S(2)}, u32[]{:S(2)}) async-start(bf16[64,3,2048]{2,1,0:T(4,128)(2,1)} %scatter_fusion), calls=%async_computation | async-start | bytes 2097152 | tf_op jit(solution)/shard_map/all_to_all | solution.py:139
  32.4 31.5 %copy-start.20 = (f32[4,2048]{1,0:T(4,128)S(1)}, f32[4,2048]{1,0:T(4,128)}, u32[]{:S(2)}) copy-start(f32[4,2048]{1,0:T(4,128)} %param.25) | copy-start | bytes 98308
  32.4 32.2 %copy-start.2 = (bf16[32,3,2048]{2,0,1:T(8,128)(2,1)S(1)}, bf16[32,3,2048]{2,0,1:T(8,128)(2,1)}, u32[]{:S(2)}) copy-start(bf16[32,3,2048]{2,0,1:T(8,128)(2,1)} %param.23) | copy-start | bytes 1179652
  32.4 32.2 %copy-start.3 = (bf16[2,32,2048]{2,1,0:T(8,128)(2,1)S(1)}, bf16[2,32,2048]{2,1,0:T(8,128)(2,1)}, u32[]{:S(2)}) copy-start(bf16[2,32,2048]{2,1,0:T(8,128)(2,1)} %param.21) | copy-start | bytes 786436
  32.4 32.2 %copy-start.19 = (f32[2048]{0:T(1024)S(1)}, f32[2048]{0:T(1024)}, u32[]{:S(2)}) copy-start(f32[2048]{0:T(1024)} %param.26) | copy-start | bytes 24580
  57.2 34.6 %all-to-all-start.2 = ((bf16[64,32,256]{2,1,0:T(8,128)(2,1)}), bf16[64,32,256]{2,1,0:T(8,128)(2,1)}, u32[]{:S(2)}, u32[]{:S(2)}) async-start(bf16[64,32,256]{2,1,0:T(8,128)(2,1)} %scatter_fusion.2), calls=%async_computation.2 | async-start | bytes 2097152 | tf_op jit(solution)/shard_map/all_to_all | solution.py:153
  63.9 50.3 %all-reduce.3.cloned.1.call-start = ((), (), s32[]{:S(2)}) async-start(), calls=%async_computation.4 | async-start | bytes 327680 | tf_op jit(solution)/shard_map/psum | solution.py:87
  64.0 0.6 copy-start.14
  64.0 0.9 copy-start.15
  64.0 0.9 copy-start.16
  64.0 0.9 copy-start.17
  64.9 1.4 copy-start.5
  68.9 47.3 %copy-start.18 = (f32[2048]{0:T(1024)S(1)}, f32[2048]{0:T(1024)}, u32[]{:S(2)}) copy-start(f32[2048]{0:T(1024)} %param.30) | copy-start | bytes 24580
  68.9 47.3 %copy-start.23 = (f32[512]{0:T(512)S(1)}, f32[512]{0:T(512)}, u32[]{:S(2)}) copy-start(f32[512]{0:T(512)} %param.28) | copy-start | bytes 6148
  91.8 42.1 %all-to-all-start.3 = ((bf16[64,32,256]{2,1,0:T(8,128)(2,1)}), bf16[64,32,256]{2,1,0:T(8,128)(2,1)}, u32[]{:S(2)}, u32[]{:S(2)}) async-start(bf16[64,32,256]{2,1,0:T(8,128)(2,1)} %scatter_fusion.3), calls=%async_computation.3 | async-start | bytes 2097152 | tf_op jit(solution)/shard_map/all_to_all | solution.py:160
  114.1 4.4 %copy-start.1 = (bf16[512,2048]{1,0:T(8,128)(2,1)S(1)}, bf16[512,2048]{1,0:T(8,128)(2,1)}, u32[]{:S(2)}) copy-start(bf16[512,2048]{1,0:T(8,128)(2,1)} %param.29) | copy-start | bytes 6291460
  114.1 4.4 %copy-start.8 = (f32[32,544]{1,0:T(8,128)S(1)}, f32[32,544]{1,0:T(8,128)}, u32[]{:S(2)}) copy-start(f32[32,544]{1,0:T(8,128)} %get-tuple-element.21) | copy-start | bytes 208900
  116.2 3.0 %copy-start.4 = (bf16[32,16,2048]{2,1,0:T(8,128)(2,1)S(1)}, bf16[32,16,2048]{2,1,0:T(8,128)(2,1)}, u32[]{:S(2)}) copy-start(bf16[32,16,2048]{2,1,0:T(8,128)(2,1)} %param.24) | copy-start | bytes 6291460
  116.2 3.0 %copy-start.13 = (f32[16,2048]{1,0:T(8,128)S(1)}, f32[16,2048]{1,0:T(8,128)}, u32[]{:S(2)}) copy-start(f32[16,2048]{1,0:T(8,128)} %param.31) | copy-start | bytes 393220
  133.9 12.3 %copy-start.12 = (s32[64,32]{1,0:T(8,128)S(1)}, s32[64,32]{1,0:T(8,128)}, u32[]{:S(2)}) copy-start(s32[64,32]{1,0:T(8,128)} %copy-done.11) | copy-start | bytes 24580
  133.9 106.7 %all-to-all-start.1 = ((bf16[64,16,2048]{2,1,0:T(8,128)(2,1)}), bf16[64,16,2048]{2,1,0:T(8,128)(2,1)}, u32[]{:S(2)}, u32[]{:S(2)}) async-start(bf16[64,16,2048]{2,1,0:T(8,128)(2,1)} %scatter_fusion.1), calls=%async_computation.1 | async-start | bytes 8388608 | tf_op jit(solution)/shard_map/all_to_all | solution.py:146
  149.4 0.7 copy-start.10
  154.9 9.7 %copy-start.6 = (f32[32,2048]{1,0:T(8,128)S(1)}, f32[32,2048]{1,0:T(8,128)}, u32[]{:S(2)}) copy-start(f32[32,2048]{1,0:T(8,128)} %get-tuple-element.19) | copy-start | bytes 786436
  154.9 9.6 %copy-start.7 = (f32[32,2048]{1,0:T(8,128)S(1)}, f32[32,2048]{1,0:T(8,128)}, u32[]{:S(2)}) copy-start(f32[32,2048]{1,0:T(8,128)} %get-tuple-element.20) | copy-start | bytes 786436
  156.4 0.7 copy-start.9
Sparse Core Ops, SparseCore 0:
  67.9 46.2 all-reduce.2
where the time goes:
time: 257 us; the launch traced here: 255 us
  waiting for transfers between devices  119 us (46%)
  local copies, waits for them, and re-layouts  46.9 us (18%)
  starting transfers between devices  39 us (15%)
  other arithmetic  21.6 us (8%)
  between operations  14.5 us (6%)
  matrix products  14.2 us (6%)
    all_to_all x1, waiting for transfers between devices, local(): lax.all_to_all(pack_slots(final_state, send_slots, total_slots), 'section...  65.5 us
    scatter x4, local copies, waits for them, and re-layouts, pack_slots(): return jnp.zeros((total_slots,) + values_in.shape[1:], values_in.dtype).a...  19.8 us
    all_to_all x1, waiting for transfers between devices, local(): lax.all_to_all(pack_slots(final_conv, send_slots, total_slots), 'section'...  18.8 us
    all_to_all x1, waiting for transfers between devices, local(): lax.all_to_all(pack_slots(key_rows, send_slots, total_slots), 'section',...  18.5 us
    psum x1, waiting for transfers between devices, local(): lax.psum(project_rows(conv_out[step_index], xproj_weight), 'tensor')  15.7 us
    all_to_all x1, starting transfers between devices, local(): lax.all_to_all(pack_slots(final_conv, send_slots, total_slots), 'section'...  13.3 us
    all_to_all x1, starting transfers between devices, local(): lax.all_to_all(pack_slots(final_state, send_slots, total_slots), 'section...  12.3 us
    all_to_all x1, starting transfers between devices, local(): lax.all_to_all(pack_slots(value_rows, send_slots, total_slots), 'section'...  6.65 us
  transfers between devices with their start and end apart: 5, of which 4 were waited for; matrix products, arithmetic and copies ran while one was open for 25% of the time, Pallas kernels for 0%

commit v1 on v0

--- a/solution.py
+++ b/solution.py
@@ -1,11 +1,18 @@
+import functools
 import math
 
 import jax
 import jax.numpy as jnp
 from jax import lax
+from jax.experimental import pallas as pl
+from jax.experimental.pallas import tpu as pltpu
 from jax.sharding import PartitionSpec as P
 
 HEAD = 128
+MESH = pl.DeviceIdType.MESH
+PLANES = 8
+RANKS = 8
+CAPS = (120, 96, 68, 36)
 
 
 epsilon = 1e-06
@@ -15,6 +22,256 @@
     return lax.dot_general(
         conv_rows, xproj_weight, (((1,), (1,)), ((), ())), preferred_element_type=jnp.float32
     )
+
+
+def route_tables(new_owner, plane):
+    requests_here = new_owner.shape[0] // (PLANES * RANKS)
+    width = RANKS * requests_here
+    owner = new_owner.reshape(PLANES, width)
+    own_plane = jnp.arange(PLANES, dtype=jnp.int32)[:, None]
+    packet = jnp.arange(width, dtype=jnp.int32)[None, :]
+    away = (owner // RANKS - own_plane) % PLANES
+    kind = jnp.where(away == 0, 7, jnp.where(away == 4, 0, jnp.where(away < 4, 4 - away, away - 1)))
+    key = kind * width + packet
+    rank = jnp.sum((key[:, None, :] < key[:, :, None]).astype(jnp.int32), axis=-1)
+    count = [jnp.sum((kind == k).astype(jnp.int32), axis=-1, keepdims=True) for k in range(7)]
+    ties = count[0]
+    ups = count[1] + count[2] + count[3]
+    downs = count[4] + count[5] + count[6]
+    ties_up = jnp.clip((ups + ties + downs + 1) // 2 - ups, 0, ties)
+    ties_down = ties - ties_up
+    goes_up = jnp.where(kind == 0, rank < ties_up, kind <= 3)
+    place = jnp.where(
+        kind == 0,
+        jnp.where(rank < ties_up, rank, rank - ties_up),
+        jnp.where(kind <= 3, rank - ties + ties_up, rank - ties - ups + ties_down),
+    )
+    hops = jnp.where(kind == 0, 4, jnp.where(kind <= 3, 4 - kind, 7 - kind))
+    starts = [0, CAPS[0], CAPS[0] + CAPS[1], CAPS[0] + CAPS[1] + CAPS[2]]
+    start = jnp.where(hops == 1, starts[0], jnp.where(hops == 2, starts[1], jnp.where(hops == 3, starts[2], starts[3])))
+    arrival = start + place + jnp.where(goes_up, 0, sum(CAPS))
+    fits = jnp.array(True)
+    for ties_here, near in ((ties_up, count[1:4]), (ties_down, count[4:7])):
+        load = ties_here
+        for hop in (3, 2, 1, 0):
+            fits = fits & jnp.all(load <= CAPS[hop])
+            if hop:
+                load = load + near[3 - hop]
+    pick = lambda rows: lax.dynamic_slice_in_dim(rows, plane, 1, 0)[0]
+    my_kind, my_up, my_place = pick(kind), pick(goes_up.astype(jnp.int32)), pick(place)
+    lane = jnp.where(my_kind == 7, -1, my_place + jnp.where(my_up == 1, 0, CAPS[0]))
+    slots = jnp.arange(2 * CAPS[0], dtype=jnp.int32)
+    lane = jnp.where((my_up == 1) & (my_place >= CAPS[0]), -1, lane)
+    send = jnp.sum(jnp.where(lane[None, :] == slots[:, None], packet, 0), axis=-1)
+    coded = jnp.where(kind == 7, packet + 65536, arrival).reshape(PLANES * RANKS, 1, requests_here)
+    mine = plane * RANKS + jnp.arange(RANKS, dtype=jnp.int32)
+    landed = new_owner.reshape(PLANES * RANKS, 1, requests_here) == mine[None, :, None]
+    found = jnp.sum(jnp.where(landed, coded, 0), axis=0).reshape(width)
+    stays = found >= 65536
+    return (
+        fits,
+        send,
+        jnp.where(stays, found - 65536, 0),
+        jnp.where(stays, 0, found),
+        stays.astype(jnp.int32),
+    )
+
+
+def migrate_kernel(count, send_tab, stay_tab, land_tab, flag_tab, *refs):
+    parts = refs[:count]
+    outs = refs[count : 2 * count]
+    spread = refs[2 * count : 3 * count]
+    queue = refs[3 * count : 4 * count]
+    ring = refs[4 * count : 5 * count]
+    gathered = refs[5 * count : 6 * count]
+    a_send, a_recv, a_self, z_send, z_recv, c_send, c_recv, c_self = refs[6 * count :]
+    section = lax.axis_index("section")
+    tensor = lax.axis_index("tensor")
+    plane = section // RANKS
+    me = section % RANKS
+    width = spread[0].shape[0]
+    each = width // RANKS
+    up = lax.rem(plane + 1, PLANES) * RANKS + me
+    down = lax.rem(plane + PLANES - 1, PLANES) * RANKS + me
+    peers = [lax.rem(me + o, RANKS) for o in range(RANKS)]
+    partner = [(plane * RANKS + p, tensor) for p in peers]
+
+    barrier = pltpu.get_barrier_semaphore()
+    for device in [partner[o] for o in range(1, RANKS)] + [(up, tensor), (down, tensor)]:
+        pl.semaphore_signal(barrier, inc=1, device_id=device, device_id_type=MESH)
+    pl.semaphore_wait(barrier, RANKS + 1)
+
+    def spread_copy(k, o):
+        return pltpu.make_async_remote_copy(
+            src_ref=parts[k].at[peers[o]],
+            dst_ref=spread[k].at[pl.ds(me * each, each)],
+            send_sem=a_send.at[k, o],
+            recv_sem=a_recv.at[k, o],
+            device_id=partner[o],
+            device_id_type=MESH,
+        )
+
+    def spread_self(k):
+        return pltpu.make_async_copy(parts[k].at[me], spread[k].at[pl.ds(me * each, each)], a_self.at[k])
+
+    starts = [0, CAPS[0], CAPS[0] + CAPS[1], CAPS[0] + CAPS[1] + CAPS[2]]
+
+    def ring_copy(k, d, h):
+        base = d * sum(CAPS)
+        if h == 0:
+            src = queue[k].at[pl.ds(d * CAPS[0], CAPS[0])]
+        else:
+            src = ring[k].at[pl.ds(base + starts[h - 1], CAPS[h])]
+        return pltpu.make_async_remote_copy(
+            src_ref=src,
+            dst_ref=ring[k].at[pl.ds(base + starts[h], CAPS[h])],
+            send_sem=z_send.at[k, d, h],
+            recv_sem=z_recv.at[k, d, h],
+            device_id=((up, down)[d], tensor),
+            device_id_type=MESH,
+        )
+
+    def gather_copy(k, o):
+        return pltpu.make_async_remote_copy(
+            src_ref=gathered[k].at[pl.ds(peers[o] * each, each)],
+            dst_ref=outs[k].at[me],
+            send_sem=c_send.at[k, o],
+            recv_sem=c_recv.at[k, o],
+            device_id=partner[o],
+            device_id_type=MESH,
+        )
+
+    def gather_self(k):
+        return pltpu.make_async_copy(gathered[k].at[pl.ds(me * each, each)], outs[k].at[me], c_self.at[k])
+
+    def begin(k):
+        for o in range(1, RANKS):
+            spread_copy(k, o).start()
+        spread_self(k).start()
+
+    def pack(k):
+        for o in range(1, RANKS):
+            spread_copy(k, o).wait_recv()
+        spread_self(k).wait()
+
+        @pl.loop(0, 2 * CAPS[0] // 8)
+        def _(s):
+            for u in range(8):
+                at = s * 8 + u
+                queue[k][at] = spread[k][send_tab[at]]
+
+        for d in range(2):
+            ring_copy(k, d, 0).start()
+
+    def forward(k, h):
+        for d in range(2):
+            ring_copy(k, d, h - 1).wait_recv()
+            ring_copy(k, d, h).start()
+
+    def unpack(k):
+        for d in range(2):
+            ring_copy(k, d, 3).wait_recv()
+
+        @pl.loop(0, width // 8)
+        def _(s):
+            for u in range(8):
+                at = s * 8 + u
+                gathered[k][at] = jnp.where(
+                    flag_tab[at] == 1, spread[k][stay_tab[at]], ring[k][land_tab[at]]
+                )
+
+        for o in range(1, RANKS):
+            gather_copy(k, o).start()
+        gather_self(k).start()
+
+    for k in range(count):
+        begin(k)
+    for step in range(count + 4):
+        for stage in (4, 3, 2, 1, 0):
+            k = step - stage
+            if 0 <= k < count:
+                if stage == 0:
+                    pack(k)
+                elif stage == 4:
+                    unpack(k)
+                else:
+                    forward(k, stage)
+    for k in range(count):
+        for o in range(1, RANKS):
+            gather_copy(k, o).wait_recv()
+        gather_self(k).wait()
+    for k in range(count):
+        for o in range(1, RANKS):
+            spread_copy(k, o).wait_send()
+            gather_copy(k, o).wait_send()
+        for d in range(2):
+            for h in range(4):
+                ring_copy(k, d, h).wait_send()
+
+
+def migrate(tables, parts):
+    count = len(parts)
+    width = RANKS * parts[0].shape[1]
+    smem = pl.BlockSpec(memory_space=pltpu.SMEM)
+    anywhere = pl.BlockSpec(memory_space=pl.ANY)
+    scratch = []
+    for slots in (width, 2 * CAPS[0], 2 * sum(CAPS), width):
+        for part in parts:
+            scratch.append(pltpu.VMEM((slots,) + part.shape[2:], part.dtype))
+    dma = pltpu.SemaphoreType.DMA
+    scratch += [
+        dma((count, RANKS)),
+        dma((count, RANKS)),
+        dma((count,)),
+        dma((count, 2, 4)),
+        dma((count, 2, 4)),
+        dma((count, RANKS)),
+        dma((count, RANKS)),
+        dma((count,)),
+    ]
+    return pl.pallas_call(
+        functools.partial(migrate_kernel, count),
+        out_shape=[jax.ShapeDtypeStruct(part.shape, part.dtype) for part in parts],
+        in_specs=[smem] * 4 + [anywhere] * count,
+        out_specs=[anywhere] * count,
+        scratch_shapes=scratch,
+        compiler_params=pltpu.CompilerParams(
+            collective_id=0, has_side_effects=True, vmem_limit_bytes=48 * 2**20
+        ),
+    )(*tables, *parts)
+
+
+def cut(final_conv, final_state, key_rows, value_rows):
+    requests, taps, channels = final_conv.shape
+    states = final_state.shape[1]
+    positions, width = key_rows.shape[1:]
+
+    def cache(rows):
+        split = rows.reshape(requests, positions // 16, 16, width // HEAD, HEAD)
+        return split.transpose(3, 1, 0, 2, 4).reshape(-1, requests, 16, HEAD)
+
+    conv = final_conv.reshape(requests, taps, RANKS, -1, HEAD).transpose(2, 0, 1, 3, 4)
+    conv = conv.reshape(RANKS, requests, -1, HEAD)
+    conv = jnp.pad(conv, ((0, 0), (0, 0), (0, 8 - conv.shape[2]), (0, 0)))
+    state = final_state.reshape(requests, states, -1, RANKS, HEAD).transpose(2, 3, 0, 1, 4)
+    return [jnp.concatenate([cache(key_rows), cache(value_rows)]), conv] + list(state)
+
+
+def join(parts, shapes):
+    caches, conv, *state = parts
+    requests, taps, channels = shapes[0]
+    positions, width = shapes[2][1:]
+
+    def cache(rows):
+        split = rows.reshape(width // HEAD, positions // 16, requests, 16, HEAD)
+        return split.transpose(2, 1, 3, 0, 4).reshape(requests, positions, width)
+
+    half = caches.shape[0] // 2
+    pieces = channels // (RANKS * HEAD)
+    conv = conv[:, :, : taps * pieces].reshape(RANKS, requests, taps, pieces, HEAD)
+    conv = conv.transpose(1, 2, 0, 3, 4).reshape(shapes[0])
+    state = jnp.stack(state).transpose(2, 3, 0, 1, 4).reshape(shapes[1])
+    return conv, state, cache(caches[:half]), cache(caches[half:])
 
 
 def slot_ranks(owners):
@@ -30,6 +287,41 @@
         jnp.zeros((total_slots,) + values_in.shape[1:], values_in.dtype)
         .at[send_slots]
         .set(values_in)
+    )
+
+
+def exchange(new_owner, arrays):
+    requests_here = arrays[0].shape[0]
+    sections = lax.axis_size("section")
+    section_index = lax.axis_index("section")
+    capacity = max(1, requests_here // sections)
+    total_slots = sections * capacity
+    owners = new_owner.reshape(sections, requests_here)
+    my_owners = lax.dynamic_slice_in_dim(owners, section_index, 1, 0)[0]
+    send_slots = my_owners * capacity + slot_ranks(my_owners)
+    ranks_all = slot_ranks(owners)
+    arriving = owners == section_index
+    sources = jnp.arange(sections, dtype=jnp.int32)[:, None]
+    recv_slots = jnp.sum(jnp.where(arriving, sources * capacity + ranks_all, 0), axis=0)
+    def select(places, options, rows):
+        chosen = (places[:, None] == jnp.arange(options)[None, :]).astype(rows.dtype)
+        flat = rows.reshape(rows.shape[0], -1)
+        picked = jnp.dot(chosen, flat, preferred_element_type=jnp.float32)
+        return picked.astype(rows.dtype).reshape((places.shape[0],) + rows.shape[1:])
+
+    return tuple(
+        select(
+            recv_slots,
+            total_slots,
+            lax.all_to_all(
+                pack_slots(array, send_slots, total_slots),
+                "section",
+                split_axis=0,
+                concat_axis=0,
+                tiled=True,
+            ),
+        )
+        for array in arrays
     )
 
 
@@ -60,17 +352,6 @@
     tap_count = conv_weight.shape[0]
     rank_width = dt_gain.shape[0]
     state_width = mamba_state.shape[1]
-    sections = lax.axis_size("section")
-    section_index = lax.axis_index("section")
-    capacity = max(1, requests_here // sections)
-    total_slots = sections * capacity
-    owners = new_owner.reshape(sections, requests_here)
-    my_owners = lax.dynamic_slice_in_dim(owners, section_index, 1, 0)[0]
-    send_slots = my_owners * capacity + slot_ranks(my_owners)
-    ranks_all = slot_ranks(owners)
-    arriving = owners == section_index
-    sources = jnp.arange(sections, dtype=jnp.int32)[:, None]
-    recv_slots = jnp.sum(jnp.where(arriving, sources * capacity + ranks_all, 0), axis=0)
     window = jnp.concatenate([conv_state, jnp.swapaxes(inner_input, 0, 1)], axis=1)
     conv_list = []
     for step_index in range(steps_count):
@@ -135,44 +416,14 @@
             "rgqc,rcgd->rgqd", weights, value_heads, preferred_element_type=jnp.float32
         )
         attended.append(mixed_out.reshape(requests_here, query_heads * HEAD).astype(jnp.bfloat16))
-    moved_conv, moved_state, moved_keys, moved_values = (
-        lax.all_to_all(
-            pack_slots(final_conv, send_slots, total_slots),
-            "section",
-            split_axis=0,
-            concat_axis=0,
-            tiled=True,
-        ),
-        lax.all_to_all(
-            pack_slots(final_state, send_slots, total_slots),
-            "section",
-            split_axis=0,
-            concat_axis=0,
-            tiled=True,
-        ),
-        lax.all_to_all(
-            pack_slots(key_rows, send_slots, total_slots),
-            "section",
-            split_axis=0,
-            concat_axis=0,
-            tiled=True,
-        ),
-        lax.all_to_all(
-            pack_slots(value_rows, send_slots, total_slots),
-            "section",
-            split_axis=0,
-            concat_axis=0,
-            tiled=True,
-        ),
-    )
-    return (
-        jnp.stack(mamba_list),
-        jnp.stack(attended),
-        jnp.take(moved_conv, recv_slots, axis=0),
-        jnp.take(moved_state, recv_slots, axis=0),
-        jnp.take(moved_keys, recv_slots, axis=0),
-        jnp.take(moved_values, recv_slots, axis=0),
-    )
+    arrays = (final_conv, final_state, key_rows, value_rows)
+    fits, *tables = route_tables(new_owner, lax.axis_index("section") // RANKS)
+    moved = lax.cond(
+        fits,
+        lambda: join(migrate(tables, cut(*arrays)), [a.shape for a in arrays]),
+        lambda: exchange(new_owner, arrays),
+    )
+    return (jnp.stack(mamba_list), jnp.stack(attended), *moved)
 
 
 def solution(mesh):

time: 257 us -> 253 us (0.984)
  Pallas kernels: 0 us -> 140 us
  waiting for transfers between devices: 119 us -> 1.55 us
  starting transfers between devices: 39 us -> 0.04 us
  other arithmetic: 21.6 us -> 29.7 us
  between operations: 14.5 us -> 19.7 us
  matrix products: 14.2 us -> 9.84 us
  local copies, waits for them, and re-layouts: 46.9 us -> 50.9 us
    pallas_call x0 -> x1, Pallas kernels: none -> 140 us  [migrate(): pl.pallas_call(functools.partial(migrate_kernel, count), out_shape=[jax.S...]
    all_to_all x4 -> x0, waiting for transfers between devices: 103 us -> none  [the longest x1 65.5 us: local(): lax.all_to_all(pack_slots(final_state, send_slots, total_slots), 'section...]
    all_to_all x4 -> x0, starting transfers between devices: 38.9 us -> none  [the longest x1 13.3 us: local(): lax.all_to_all(pack_slots(final_conv, send_slots, total_slots), 'section'...]
    scatter x4 -> x0, local copies, waits for them, and re-layouts: 19.8 us -> none  [pack_slots(): return jnp.zeros((total_slots,) + values_in.shape[1:], values_in.dtype).a...]
    psum x1, waiting for transfers between devices: 15.7 us -> 1.53 us  [local(): lax.psum(project_rows(conv_out[step_index], xproj_weight), 'tensor')]
    gather x4 -> x0, local copies, waits for them, and re-layouts: 10 us -> none  [the longest x1 4.19 us: local(): jnp.take(moved_state, recv_slots, axis=0)]
    reshape x2 -> x13, local copies, waits for them, and re-layouts: 0.98 us -> 10.3 us  [the longest x1 4.15 us: join(): state = jnp.stack(state).transpose(2, 3, 0, 1, 4).reshape(shapes[1])]
    sub x0 -> x6, local copies, waits for them, and re-layouts: none -> 7.09 us  [the longest x2 2.62 us: route_tables(): rank - ties + ties_up]
  transfers between devices with their start and end apart: 5 -> 1, of which waited for: 4 -> 1; matrix products, arithmetic and copies ran while one was open for 25% -> 16% of each run, Pallas kernels for 0% -> 0%
where the time goes in v1:
time: 253 us; the launch traced here: 252 us
  Pallas kernels  140 us (55%)
  local copies, waits for them, and re-layouts  50.9 us (20%)
  other arithmetic  29.7 us (12%)
  between operations  19.7 us (8%)
  matrix products  9.84 us (4%)
    pallas_call x1, Pallas kernels, migrate(): pl.pallas_call(functools.partial(migrate_kernel, count), out_shape=[jax.S...  140 us
    reduce_sum x1, other arithmetic, local(): jnp.sum(hidden * output_gain[:, :, None], axis=1) + skip_gain * inputs_now  6.06 us
  transfers between devices with their start and end apart: 1, of which 1 were waited for; matrix products, arithmetic and copies ran while one was open for 16% of the time, Pallas kernels for 0%

profile of v1, /device:TPU:1, one launch (start us, length us, event | category | flops | bytes accessed | tf_op | source)
XLA Modules:
  0.0 252.0 jit_solution(18362875540048943691)
XLA Ops:
  8.3 1.5 multiply_convert_fusion.1
  9.8 1.4 fusion.98
  11.3 1.4 fusion.99
  19.9 3.0 %convolution_convert_fusion.5 = bf16[32,2,8,128]{3,2,1,0:T(8,128)(2,1)} fusion(bf16[32,4,2,8,128]{4,3,2,1,0:T(8,128)(2,1)} %get-tuple-element.230, f32[32,2,8]{2,1,0:T(2,128)S(1)} %fusion.97, f32[32,2,8,32]{3,2,1,0:T(8,128)} %copy-done.18), kind=kOutput, calls=%fused_computation.63 | convolution fusion | flops 4309535 | bytes 722944 | tf_op jit(solution)/shard_map/rgqc,rcgd->rgqd/dot_general | solution.py:415
  22.9 1.7 convert_element_type.301
  26.0 1.3 compare_reduce_fusion
  33.7 1.4 convert_reduce_fusion
  35.8 1.3 select_convert_fusion
  37.1 1.3 add.722
  38.4 1.3 add.723
  39.8 1.3 sub.230
  43.6 1.4 sub.227
  45.0 1.3 lt.123
  46.2 1.3 lt.124
  48.2 1.3 sub.218
  49.5 1.4 copy.72
  50.9 1.5 fusion.78
  52.4 1.4 copy.73
  53.9 1.6 select_reduce_fusion.4
  55.5 1.3 reshape.1184
  56.8 1.7 pad_maximum_fusion.3
  59.7 1.5 all-reduce.4.cloned.1.call-done
  63.2 1.7 fusion.92
  65.6 6.1 %multiply_reduce_fusion.1 = (f32[32,2048]{1,0:T(8,128)S(1)}, f32[32,2048]{1,0:T(8,128)S(1)}, bf16[32,16,2048]{2,1,0:T(8,128)(2,1)S(1)}) fusion(bf16[32,16,2048]{2,1,0:T(8,128)(2,1)S(1)} %copy-done.10, f32[32,16]{1,0:T(8,128)S(1)} %get-tuple-element.264, f32[32,16]{1,0:T(8,128)S(1)} %get-tuple-element.265, f32[32,2048]{1,0:T(8,128)S(1)} %get-tuple-element.237, ...), kind=kLoop, calls=%fused_computation.46 | loop fusion | flops 14548992 | bytes 5906432 | tf_op jit(solution)/shard_map/reduce_sum | solution.py:385
  73.8 169.6 %conditional.1 = (bf16[32,3,2048]{2,0,1:T(8,128)(2,1)}, bf16[32,16,2048]{2,1,0:T(8,128)(2,1)}, bf16[32,32,256]{2,1,0:T(8,128)(2,1)}, bf16[32,32,256]{2,1,0:T(8,128)(2,1)S(1)}) conditional(s32[]{:T(128)} %convert_element_type.312, (s32[2048]{0:T(1024)}, bf16[32,3,2048]{2,0,1:T(8,128)(2,1)}, bf16[32,16,2048]{2,1,0:T(8,128)(2,1)S(1)}, ...), branch_computations={%region_27.35_spmd, %region_35.37_spmd} | conditional | flops 228544576 | bytes 72159472 | solution.py:421
  77.4 2.7 %and_select_fusion = s32[1,256]{1,0:T(1,128)S(1)} fusion(s32[8,256]{1,0:T(8,128)S(1)} %get-tuple-element.135, s32[]{:T(128)S(6)} %select_n.274, s32[8,256]{1,0:T(8,128)} %get-tuple-element.125, pred[8,256]{1,0:T(8,128)(4,1)} %get-tuple-element.131, pred[8,256]{1,0:T(8,128)(4,1)} %get-tuple-element.128, pred[8,256]{1,0:T(8,128)(4,1)} %get-tuple-element.127, ...), kind=kLoop, calls=%fused_computation.14 | loop fusion | flops 4096 | bytes 5904 | tf_op jit(solution)/shard_map/jit(_where)/select_n | solution.py:64
  83.7 2.2 copy.75
  86.5 1.7 slice_bitcast_fusion
  88.2 140.2 %branch_1_fun.1 = (bf16[8,32,16,128]{3,2,1,0:T(8,128)(2,1)S(1)}, bf16[8,32,8,128]{3,2,1,0:T(8,128)(2,1)S(1)}, bf16[8,32,16,128]{3,2,1,0:T(8,128)(2,1)S(1)}, bf16[8,32,16,128]{3,2,1,0:T(8,128)(2,1)S(1)}) custom-call(s32[240]{0:T(256)S(1)} %select_reduce_fusion.send_tab, s32[256]{0:T(256)S(1)} %get-tuple-element.222.stay_tab, ...), custom_call_target="tpu_custom_call" | custom-call | tf_op jit(solution)/shard_map/cond/branch_1_fun/pallas_call | solution.py:232
  230.4 2.0 reshape.1167
  232.7 3.8 %copy.61 = bf16[32,16,2,8,128]{4,3,2,1,0:T(8,128)(2,1)} copy(bf16[32,16,2,8,128]{4,1,0,3,2:T(8,128)(2,1)S(1)} %maximum_bitcast_fusion) | data formatting | bytes 4194304 | tf_op jit(solution)/shard_map/cond/branch_1_fun/transpose | solution.py:273
  236.4 4.2 %reshape.1168 = bf16[32,16,2048]{2,1,0:T(8,128)(2,1)} reshape(bf16[32,16,2,8,128]{4,3,2,1,0:T(8,128)(2,1)} %copy.61) | data formatting | bytes 4194304 | tf_op jit(solution)/shard_map/cond/branch_1_fun/reshape | solution.py:273
  (146 shorter events, 35.0 us)
Async XLA Ops:
  7.2 2.6 %copy-start = (bf16[544,2048]{1,0:T(8,128)(2,1)S(1)}, bf16[544,2048]{1,0:T(8,128)(2,1)}, u32[]{:S(2)}) copy-start(bf16[544,2048]{1,0:T(8,128)(2,1)} %param.27) | copy-start | bytes 6684676
  7.2 54.0 %all-reduce.4.cloned.1.call-start = ((), (), s32[]{:S(2)}) async-start(), calls=%async_computation.4 | async-start | bytes 327680 | tf_op jit(solution)/shard_map/psum | solution.py:368
  9.8 2.9 %copy-start.11 = (bf16[32,2048]{1,0:T(8,128)(2,1)}, bf16[32,2048]{1,0:T(8,128)(2,1)S(1)}, u32[]{:S(2)}) copy-start(bf16[32,2048]{1,0:T(8,128)(2,1)S(1)} %get-tuple-element.226) | copy-start | bytes 393220
  9.8 2.9 %copy-start.13 = (bf16[32,2048]{1,0:T(8,128)(2,1)}, bf16[32,2048]{1,0:T(8,128)(2,1)S(1)}, u32[]{:S(2)}) copy-start(bf16[32,2048]{1,0:T(8,128)(2,1)S(1)} %get-tuple-element.227) | copy-start | bytes 393220
  9.8 2.9 %copy-start.7 = (bf16[32,3,2048]{2,0,1:T(8,128)(2,1)S(1)}, bf16[32,3,2048]{2,0,1:T(8,128)(2,1)}, u32[]{:S(2)}) copy-start(bf16[32,3,2048]{2,0,1:T(8,128)(2,1)} %param.23) | copy-start | bytes 1179652
  9.8 2.9 %copy-start.9 = (bf16[2,32,2048]{2,1,0:T(8,128)(2,1)S(1)}, bf16[2,32,2048]{2,1,0:T(8,128)(2,1)}, u32[]{:S(2)}) copy-start(bf16[2,32,2048]{2,1,0:T(8,128)(2,1)} %param.21) | copy-start | bytes 786436
  11.2 2.3 copy-start.30
  11.2 3.6 %copy-start.19 = (bf16[2,32,2048]{2,1,0:T(8,128)(2,1)S(1)}, bf16[2,32,2048]{2,1,0:T(8,128)(2,1)}, u32[]{:S(2)}) copy-start(bf16[2,32,2048]{2,1,0:T(8,128)(2,1)} %param.33) | copy-start | bytes 786436
  11.3 3.6 %copy-start.41 = (s32[32]{0:T(128)S(1)}, s32[32]{0:T(128)}, u32[]{:S(2)}) copy-start(s32[32]{0:T(128)} %param.38) | copy-start | bytes 388
  11.3 3.7 %copy-start.33 = (bf16[2,32,256]{2,1,0:T(8,128)(2,1)S(1)}, bf16[2,32,256]{2,1,0:T(8,128)(2,1)}, u32[]{:S(2)}) copy-start(bf16[2,32,256]{2,1,0:T(8,128)(2,1)} %param.37) | copy-start | bytes 98308
  11.3 3.7 %copy-start.34 = (bf16[2,32,256]{2,1,0:T(8,128)(2,1)S(1)}, bf16[2,32,256]{2,1,0:T(8,128)(2,1)}, u32[]{:S(2)}) copy-start(bf16[2,32,256]{2,1,0:T(8,128)(2,1)} %param.36) | copy-start | bytes 98308
  12.7 2.3 copy-start.14
  12.7 2.3 copy-start.15
  19.6 43.5 %copy-start.5 = (bf16[512,2048]{1,0:T(8,128)(2,1)S(1)}, bf16[512,2048]{1,0:T(8,128)(2,1)}, u32[]{:S(2)}) copy-start(bf16[512,2048]{1,0:T(8,128)(2,1)} %param.29) | copy-start | bytes 6291460
  22.9 42.0 %copy-start.12 = (bf16[32,2048]{1,0:T(8,128)(2,1)S(1)}, bf16[32,2048]{1,0:T(8,128)(2,1)}, u32[]{:S(2)}) copy-start(bf16[32,2048]{1,0:T(8,128)(2,1)} %copy-done.11) | copy-start | bytes 393220
  26.0 2.6 %copy-start.39 = (s32[8]{0:T(128)}, s32[8]{0:T(128)S(1)}, u32[]{:S(2)}) copy-start(s32[8]{0:T(128)S(1)} %get-tuple-element.215) | copy-start | bytes 100
  61.2 3.7 %copy-start.17 = (f32[32,544]{1,0:T(8,128)S(1)}, f32[32,544]{1,0:T(8,128)}, u32[]{:S(2)}) copy-start(f32[32,544]{1,0:T(8,128)} %get-tuple-element.204) | copy-start | bytes 208900
  61.2 3.7 %copy-start.31 = (f32[2048]{0:T(1024)S(1)}, f32[2048]{0:T(1024)}, u32[]{:S(2)}) copy-start(f32[2048]{0:T(1024)} %param.30) | copy-start | bytes 24580
  61.2 3.7 %copy-start.38 = (f32[512]{0:T(512)S(1)}, f32[512]{0:T(512)}, u32[]{:S(2)}) copy-start(f32[512]{0:T(512)} %param.28) | copy-start | bytes 6148
  63.2 2.4 copy-start.10
  63.2 2.4 copy-start.21
  65.5 6.2 %copy-start.8 = (bf16[32,3,2048]{2,0,1:T(8,128)(2,1)S(1)}, bf16[32,3,2048]{2,0,1:T(8,128)(2,1)}, u32[]{:S(2)}) copy-start(bf16[32,3,2048]{2,0,1:T(8,128)(2,1)} %param.23) | copy-start | bytes 1179652
  65.5 6.2 %copy-start.20 = (bf16[2,32,2048]{2,1,0:T(8,128)(2,1)S(1)}, bf16[2,32,2048]{2,1,0:T(8,128)(2,1)}, u32[]{:S(2)}) copy-start(bf16[2,32,2048]{2,1,0:T(8,128)(2,1)} %param.22) | copy-start | bytes 786436
  65.6 6.2 %copy-start.23 = (f32[1,2048]{1,0:T(1,128)S(1)}, f32[1,2048]{1,0:T(1,128)}, u32[]{:S(2)}) copy-start(f32[1,2048]{1,0:T(1,128)} %copy-done.22) | copy-start | bytes 24580
  65.6 6.2 %copy-start.25 = (f32[1,2048]{1,0:T(1,128)S(1)}, f32[1,2048]{1,0:T(1,128)}, u32[]{:S(2)}) copy-start(f32[1,2048]{1,0:T(1,128)} %copy-done.24) | copy-start | bytes 24580
  65.6 6.2 %copy-start.27 = (f32[1,2048]{1,0:T(1,128)S(1)}, f32[1,2048]{1,0:T(1,128)}, u32[]{:S(2)}) copy-start(f32[1,2048]{1,0:T(1,128)} %copy-done.26) | copy-start | bytes 24580
  65.6 6.2 %copy-start.29 = (f32[1,2048]{1,0:T(1,128)S(1)}, f32[1,2048]{1,0:T(1,128)}, u32[]{:S(2)}) copy-start(f32[1,2048]{1,0:T(1,128)} %copy-done.28) | copy-start | bytes 24580
  65.6 6.2 %copy-start.32 = (f32[2048]{0:T(1024)S(1)}, f32[2048]{0:T(1024)}, u32[]{:S(2)}) copy-start(f32[2048]{0:T(1024)} %param.26) | copy-start | bytes 24580
  65.6 6.2 %copy-start.37 = (f32[2048]{0:T(1024)S(1)}, f32[2048]{0:T(1024)}, u32[]{:S(2)}) copy-start(f32[2048]{0:T(1024)} %param.32) | copy-start | bytes 24580
  73.8 6.3 %copy-start.4 = (bf16[32,16,2048]{2,1,0:T(8,128)(2,1)}, bf16[32,16,2048]{2,1,0:T(8,128)(2,1)S(1)}, u32[]{:S(2)}) copy-start(bf16[32,16,2048]{2,1,0:T(8,128)(2,1)S(1)} %get-tuple-element.144) | copy-start | bytes 6291460 | tf_op jit(solution)/shard_map/cond
  229.3 3.1 %copy-start.3 = (bf16[8,32,16,128]{3,2,1,0:T(8,128)(2,1)S(1)}, bf16[8,32,16,128]{3,2,1,0:T(8,128)(2,1)}, u32[]{:S(2)}) copy-start(bf16[8,32,16,128]{3,2,1,0:T(8,128)(2,1)} %copy-done.2) | copy-start | bytes 3145732 | tf_op jit(solution)/shard_map/cond
  243.4 1.8 copy-start.1
  (11 other events, 13.1 us)
Sparse Core Ops, SparseCore 0:
  12.8 48.3 all-reduce.3

commit v2 on v1

--- a/solution.py
+++ b/solution.py
@@ -13,80 +13,137 @@
 PLANES = 8
 RANKS = 8
 CAPS = (120, 96, 68, 36)
+STARTS = (0, CAPS[0], CAPS[0] + CAPS[1], CAPS[0] + CAPS[1] + CAPS[2])
 
 
 epsilon = 1e-06
 
 
-def project_rows(conv_rows, xproj_weight):
-    return lax.dot_general(
-        conv_rows, xproj_weight, (((1,), (1,)), ((), ())), preferred_element_type=jnp.float32
-    )
-
-
-def route_tables(new_owner, plane):
-    requests_here = new_owner.shape[0] // (PLANES * RANKS)
-    width = RANKS * requests_here
-    owner = new_owner.reshape(PLANES, width)
-    own_plane = jnp.arange(PLANES, dtype=jnp.int32)[:, None]
-    packet = jnp.arange(width, dtype=jnp.int32)[None, :]
-    away = (owner // RANKS - own_plane) % PLANES
+def table_kernel(owner_ref, out_ref, mem_ref):
+    planes, width = owner_ref.shape
+    each = width // RANKS
+    plane = lax.axis_index("section") // RANKS
+    owner = owner_ref[...]
+    own_plane = lax.broadcasted_iota(jnp.int32, (planes, width), 0)
+    packet = lax.broadcasted_iota(jnp.int32, (planes, width), 1)
+    away = (owner // RANKS - own_plane + PLANES) % PLANES
     kind = jnp.where(away == 0, 7, jnp.where(away == 4, 0, jnp.where(away < 4, 4 - away, away - 1)))
     key = kind * width + packet
-    rank = jnp.sum((key[:, None, :] < key[:, :, None]).astype(jnp.int32), axis=-1)
-    count = [jnp.sum((kind == k).astype(jnp.int32), axis=-1, keepdims=True) for k in range(7)]
+    key_columns = key.T
+    rank = jnp.concatenate(
+        [
+            jnp.sum((key_columns[:, p : p + 1] < key[p : p + 1, :]).astype(jnp.int32), axis=0, keepdims=True)
+            for p in range(planes)
+        ]
+    )
+    count = [jnp.sum((kind == k).astype(jnp.int32), axis=1, keepdims=True) for k in range(7)]
     ties = count[0]
     ups = count[1] + count[2] + count[3]
     downs = count[4] + count[5] + count[6]
-    ties_up = jnp.clip((ups + ties + downs + 1) // 2 - ups, 0, ties)
+    ties_up = jnp.minimum(jnp.maximum((ups + ties + downs + 1) // 2 - ups, 0), ties)
     ties_down = ties - ties_up
-    goes_up = jnp.where(kind == 0, rank < ties_up, kind <= 3)
+    tied_up = rank < ties_up
+    goes_up = jnp.where(kind == 0, tied_up.astype(jnp.int32), (kind <= 3).astype(jnp.int32))
     place = jnp.where(
         kind == 0,
-        jnp.where(rank < ties_up, rank, rank - ties_up),
+        jnp.where(tied_up, rank, rank - ties_up),
         jnp.where(kind <= 3, rank - ties + ties_up, rank - ties - ups + ties_down),
     )
     hops = jnp.where(kind == 0, 4, jnp.where(kind <= 3, 4 - kind, 7 - kind))
-    starts = [0, CAPS[0], CAPS[0] + CAPS[1], CAPS[0] + CAPS[1] + CAPS[2]]
-    start = jnp.where(hops == 1, starts[0], jnp.where(hops == 2, starts[1], jnp.where(hops == 3, starts[2], starts[3])))
-    arrival = start + place + jnp.where(goes_up, 0, sum(CAPS))
-    fits = jnp.array(True)
+    start = jnp.where(
+        hops == 1, STARTS[0], jnp.where(hops == 2, STARTS[1], jnp.where(hops == 3, STARTS[2], STARTS[3]))
+    )
+    arrival = start + place + jnp.where(goes_up == 1, 0, sum(CAPS))
+    over = jnp.zeros_like(ties)
     for ties_here, near in ((ties_up, count[1:4]), (ties_down, count[4:7])):
         load = ties_here
         for hop in (3, 2, 1, 0):
-            fits = fits & jnp.all(load <= CAPS[hop])
+            over = over + (load > CAPS[hop]).astype(jnp.int32)
             if hop:
                 load = load + near[3 - hop]
-    pick = lambda rows: lax.dynamic_slice_in_dim(rows, plane, 1, 0)[0]
-    my_kind, my_up, my_place = pick(kind), pick(goes_up.astype(jnp.int32)), pick(place)
-    lane = jnp.where(my_kind == 7, -1, my_place + jnp.where(my_up == 1, 0, CAPS[0]))
-    slots = jnp.arange(2 * CAPS[0], dtype=jnp.int32)
-    lane = jnp.where((my_up == 1) & (my_place >= CAPS[0]), -1, lane)
-    send = jnp.sum(jnp.where(lane[None, :] == slots[:, None], packet, 0), axis=-1)
-    coded = jnp.where(kind == 7, packet + 65536, arrival).reshape(PLANES * RANKS, 1, requests_here)
-    mine = plane * RANKS + jnp.arange(RANKS, dtype=jnp.int32)
-    landed = new_owner.reshape(PLANES * RANKS, 1, requests_here) == mine[None, :, None]
-    found = jnp.sum(jnp.where(landed, coded, 0), axis=0).reshape(width)
+    over = jnp.sum(over, axis=0, keepdims=True)
+
+    lane = jnp.where(kind == 7, -1, jnp.where(goes_up == 1, place, place + CAPS[0]))
+    mem_ref[...] = jnp.where((goes_up == 1) & (place >= CAPS[0]), -1, lane)
+    mine = jnp.broadcast_to(mem_ref[pl.ds(plane, 1), :], (8, width)).T[:, :1]
+    slot = lax.broadcasted_iota(jnp.int32, (width, width), 1)
+    number = lax.broadcasted_iota(jnp.int32, (width, width), 0)
+    send = jnp.sum(jnp.where(mine == slot, number, 0), axis=0, keepdims=True)
+
+    coded = jnp.where(kind == 7, packet + 65536, arrival)
+    spot = lax.broadcasted_iota(jnp.int32, (1, width), 1) // each
+    found = jnp.zeros((1, width), jnp.int32)
+    for r in range(RANKS):
+        row = jnp.sum(jnp.where(owner == plane * RANKS + r, coded, 0), axis=0, keepdims=True)
+        shift = each
+        while shift < width:
+            row = row + pltpu.roll(row, shift, 1)
+            shift *= 2
+        found = jnp.where(spot == r, row, found)
     stays = found >= 65536
-    return (
-        fits,
-        send,
-        jnp.where(stays, found - 65536, 0),
-        jnp.where(stays, 0, found),
-        stays.astype(jnp.int32),
-    )
-
-
-def migrate_kernel(count, send_tab, stay_tab, land_tab, flag_tab, *refs):
-    parts = refs[:count]
-    outs = refs[count : 2 * count]
-    spread = refs[2 * count : 3 * count]
-    queue = refs[3 * count : 4 * count]
-    ring = refs[4 * count : 5 * count]
-    gathered = refs[5 * count : 6 * count]
-    a_send, a_recv, a_self, z_send, z_recv, c_send, c_recv, c_self = refs[6 * count :]
+    out_ref[...] = jnp.concatenate(
+        [
+            send,
+            jnp.where(stays, found - 65536, 0),
+            jnp.where(stays, 0, found),
+            stays.astype(jnp.int32),
+            jnp.broadcast_to((over == 0).astype(jnp.int32), (4, width)),
+        ]
+    )
+
+
+def route_tables(new_owner):
+    width = new_owner.shape[0] // PLANES
+    return pl.pallas_call(
+        table_kernel,
+        out_shape=jax.ShapeDtypeStruct((8, width), jnp.int32),
+        in_specs=[pl.BlockSpec(memory_space=pltpu.VMEM)],
+        out_specs=pl.BlockSpec(memory_space=pltpu.VMEM),
+        scratch_shapes=[pltpu.VMEM((PLANES, width), jnp.int32)],
+    )(new_owner.reshape(PLANES, width))
+
+
+def silu(v):
+    return v * (1.0 / (1.0 + jnp.exp(-v)))
+
+
+LOADS = (
+    "key_cache",
+    "value_cache",
+    "key_new",
+    "value_new",
+    "window",
+    "conv_weight",
+    "conv_bias",
+    "xproj",
+    "query",
+    "lengths",
+    "dt_gain",
+    "dtproj",
+    "dt_bias",
+    "decay",
+    "state",
+    "gate",
+    "skip",
+)
+
+
+def step_kernel(shapes, tab, kv_len, conv_in, *refs):
+    total = len(LOADS)
+    hbm = dict(zip(LOADS, refs[:total]))
+    out_mamba, out_attn, out_conv, out_state, out_keys, out_values = refs[total : total + 6]
+    rest = list(refs[total + 6 :])
+    take = lambda n: [rest.pop(0) for _ in range(n)]
+    mem = dict(zip(LOADS, take(total)))
+    count = len(shapes)
+    spread, queue, ring, gathered = take(count), take(count), take(count), take(count)
+    caches, *states = take(count - 1)
+    key_fresh, value_fresh, conv_out, low_parts, gain_parts, delta, push, reading, gains, mamba, attn = take(11)
+    in_sem, a_send, a_recv, a_self, z_send, z_recv, c_send, c_recv, c_self, p_send, p_recv, o_sem = take(12)
+
     section = lax.axis_index("section")
     tensor = lax.axis_index("tensor")
+    tensors = lax.axis_size("tensor")
     plane = section // RANKS
     me = section % RANKS
     width = spread[0].shape[0]
@@ -95,15 +152,31 @@
     down = lax.rem(plane + PLANES - 1, PLANES) * RANKS + me
     peers = [lax.rem(me + o, RANKS) for o in range(RANKS)]
     partner = [(plane * RANKS + p, tensor) for p in peers]
+    beside = [(section, lax.rem(tensor + o, tensors)) for o in range(tensors)]
+
+    def load(name):
+        return pltpu.make_async_copy(hbm[name], mem[name], in_sem.at[LOADS.index(name)])
+
+    for name in LOADS:
+        load(name).start()
 
     barrier = pltpu.get_barrier_semaphore()
-    for device in [partner[o] for o in range(1, RANKS)] + [(up, tensor), (down, tensor)]:
+    friends = partner[1:] + [(up, tensor), (down, tensor)] + beside[1:]
+    for device in friends:
         pl.semaphore_signal(barrier, inc=1, device_id=device, device_id_type=MESH)
-    pl.semaphore_wait(barrier, RANKS + 1)
+    pl.semaphore_wait(barrier, len(friends))
+
+    def lanes(at, size):
+        return pl.ds(pl.multiple_of(at, HEAD), size)
+
+    def part(k, rank):
+        if k == 0:
+            return conv_in.at[:, :, lanes(rank * 2 * HEAD, 2 * HEAD)]
+        return (caches if k == 1 else states[k - 2]).at[rank]
 
     def spread_copy(k, o):
         return pltpu.make_async_remote_copy(
-            src_ref=parts[k].at[peers[o]],
+            src_ref=part(k, peers[o]),
             dst_ref=spread[k].at[pl.ds(me * each, each)],
             send_sem=a_send.at[k, o],
             recv_sem=a_recv.at[k, o],
@@ -112,37 +185,46 @@
         )
 
     def spread_self(k):
-        return pltpu.make_async_copy(parts[k].at[me], spread[k].at[pl.ds(me * each, each)], a_self.at[k])
-
-    starts = [0, CAPS[0], CAPS[0] + CAPS[1], CAPS[0] + CAPS[1] + CAPS[2]]
+        return pltpu.make_async_copy(part(k, me), spread[k].at[pl.ds(me * each, each)], a_self.at[k])
 
     def ring_copy(k, d, h):
         base = d * sum(CAPS)
         if h == 0:
             src = queue[k].at[pl.ds(d * CAPS[0], CAPS[0])]
         else:
-            src = ring[k].at[pl.ds(base + starts[h - 1], CAPS[h])]
+            src = ring[k].at[pl.ds(base + STARTS[h - 1], CAPS[h])]
         return pltpu.make_async_remote_copy(
             src_ref=src,
-            dst_ref=ring[k].at[pl.ds(base + starts[h], CAPS[h])],
+            dst_ref=ring[k].at[pl.ds(base + STARTS[h], CAPS[h])],
             send_sem=z_send.at[k, d, h],
             recv_sem=z_recv.at[k, d, h],
             device_id=((up, down)[d], tensor),
             device_id_type=MESH,
         )
 
-    def gather_copy(k, o):
+    def home(k, values):
+        if k == 0:
+            return out_conv.at[:, :, lanes(me * 2 * HEAD, 2 * HEAD)]
+        if k == 1:
+            at = lax.rem(me, 4)
+            rows = pl.ds(pl.multiple_of(lax.rem(at, 2) * 16, 16), 16)
+            return (out_values if values else out_keys).at[:, rows, lanes(at // 2 * HEAD, HEAD)]
+        return out_state.at[:, :, lanes((k - 2) * RANKS * HEAD + me * HEAD, HEAD)]
+
+    def gather_copy(k, o, values=False):
         return pltpu.make_async_remote_copy(
             src_ref=gathered[k].at[pl.ds(peers[o] * each, each)],
-            dst_ref=outs[k].at[me],
+            dst_ref=home(k, values),
             send_sem=c_send.at[k, o],
             recv_sem=c_recv.at[k, o],
             device_id=partner[o],
             device_id_type=MESH,
         )
 
-    def gather_self(k):
-        return pltpu.make_async_copy(gathered[k].at[pl.ds(me * each, each)], outs[k].at[me], c_self.at[k])
+    def gather_self(k, values=False):
+        return pltpu.make_async_copy(
+            gathered[k].at[pl.ds(me * each, each)], home(k, values), c_self.at[k]
+        )
 
     def begin(k):
         for o in range(1, RANKS):
@@ -158,7 +240,7 @@
         def _(s):
             for u in range(8):
                 at = s * 8 + u
-                queue[k][at] = spread[k][send_tab[at]]
+                queue[k][at] = spread[k][tab[0, at]]
 
         for d in range(2):
             ring_copy(k, d, 0).start()
@@ -177,29 +259,249 @@
             for u in range(8):
                 at = s * 8 + u
                 gathered[k][at] = jnp.where(
-                    flag_tab[at] == 1, spread[k][stay_tab[at]], ring[k][land_tab[at]]
+                    tab[3, at] == 1, spread[k][tab[1, at]], ring[k][tab[2, at]]
                 )
 
-        for o in range(1, RANKS):
-            gather_copy(k, o).start()
-        gather_self(k).start()
-
-    for k in range(count):
-        begin(k)
-    for step in range(count + 4):
-        for stage in (4, 3, 2, 1, 0):
-            k = step - stage
-            if 0 <= k < count:
-                if stage == 0:
-                    pack(k)
-                elif stage == 4:
-                    unpack(k)
-                else:
-                    forward(k, stage)
+        def send(values):
+            for o in range(1, RANKS):
+                gather_copy(k, o, values).start()
+            gather_self(k, values).start()
+
+        if k == 1:
+            pl.when(me < 4)(lambda: send(False))
+            pl.when(me >= 4)(lambda: send(True))
+        else:
+            send(False)
+
+    requests = each
+    channels = conv_out.shape[1]
+    steps = conv_out.shape[0] // requests
+
+    def update_caches():
+        load("key_new").wait()
+        load("value_new").wait()
+        key_fresh[...] = mem["key_new"][...].astype(jnp.float32)
+        value_fresh[...] = mem["value_new"][...].astype(jnp.float32)
+        load("key_cache").wait()
+        load("value_cache").wait()
+
+        @pl.loop(0, requests // 8)
+        def _(block):
+            ats = [pl.ds(pl.multiple_of(s * requests + block * 8, 8), 8) for s in range(steps)]
+            for base, cache, fresh in ((0, mem["key_cache"], key_fresh), (4, mem["value_cache"], value_fresh)):
+                for g in range(2):
+                    cols = slice(g * HEAD, (g + 1) * HEAD)
+                    new = [fresh[at, cols] for at in ats]
+                    for u in range(8):
+                        r = block * 8 + u
+                        for p in range(2):
+                            rows = lax.broadcasted_iota(jnp.int32, (16, HEAD), 0) + p * 16
+                            tile = cache[r, p * 16 : p * 16 + 16, cols].astype(jnp.float32)
+                            for s in range(steps):
+                                tile = jnp.where(rows == kv_len[r] + s, new[s][u : u + 1], tile)
+                            caches[base + g * 2 + p, r] = tile.astype(caches.dtype)
+
+    def convolve():
+        load("window").wait()
+        load("conv_weight").wait()
+        load("conv_bias").wait()
+        taps = mem["conv_weight"].shape[0]
+
+        @pl.loop(0, channels // 256)
+        def _(b):
+            cols = pl.ds(pl.multiple_of(b * 256, 256), 256)
+            for s in range(steps):
+                total_in = mem["conv_bias"][:, cols]
+                for k in range(taps):
+                    total_in = total_in + mem["conv_weight"][k : k + 1, cols] * mem["window"][
+                        s + k, :, cols
+                    ].astype(jnp.float32)
+                conv_out[s * requests : (s + 1) * requests, cols] = silu(total_in).astype(conv_out.dtype)
+
+    def share_copies(o):
+        return [
+            pltpu.make_async_remote_copy(
+                src_ref=buf.at[tensor],
+                dst_ref=buf.at[tensor],
+                send_sem=p_send.at[n, o],
+                recv_sem=p_recv.at[n, o],
+                device_id=beside[o],
+                device_id_type=MESH,
+            )
+            for n, buf in enumerate((low_parts, gain_parts))
+        ]
+
+    rank_width = low_parts.shape[2]
+    state_width = gains.shape[1] // 2
+    nt = (((1,), (1,)), ((), ()))
+
+    def project():
+        load("xproj").wait()
+        low_parts[tensor] = lax.dot_general(
+            conv_out[...], mem["xproj"][:rank_width], nt, preferred_element_type=jnp.float32
+        )
+        gain_parts[tensor, :, : steps * requests] = lax.dot_general(
+            mem["xproj"][rank_width:], conv_out[...], nt, preferred_element_type=jnp.float32
+        )
+        for o in range(1, tensors):
+            for copy in share_copies(o):
+                copy.start()
+
+    def rates():
+        for o in range(1, tensors):
+            for copy in share_copies(o):
+                copy.wait_recv()
+        low = low_parts[0]
+        both = gain_parts[0]
+        for t in range(1, tensors):
+            low = low + low_parts[t]
+            both = both + gain_parts[t]
+        load("dt_gain").wait()
+        load("dtproj").wait()
+        load("dt_bias").wait()
+        mean = jnp.mean(low * low, axis=-1, keepdims=True)
+        scaled = (low * lax.rsqrt(mean + epsilon) * mem["dt_gain"][...]).astype(conv_out.dtype)
+        for b in range(channels // 512):
+            cols = slice(b * 512, (b + 1) * 512)
+            rate = (
+                jnp.dot(scaled, mem["dtproj"][:, cols], preferred_element_type=jnp.float32)
+                + mem["dt_bias"][:, cols]
+            )
+            rate = jnp.maximum(rate, 0.0) + jnp.log1p(jnp.exp(-jnp.abs(rate)))
+            delta[:, cols] = rate
+            push[:, cols] = rate * conv_out[:, cols].astype(jnp.float32)
+        for c in range(steps * requests):
+            gains[c] = jnp.broadcast_to(both[:, c : c + 1], (2 * state_width, HEAD))
+
+    def recur(half):
+        @pl.loop(0, requests // 8 * 4)
+        def _(turn):
+            block, b = turn // 4, lax.rem(turn, 4)
+            cols = pl.ds(pl.multiple_of(half * RANKS * HEAD + b * 256, 256), 256)
+            ats = [pl.ds(pl.multiple_of(s * requests + block * 8, 8), 8) for s in range(steps)]
+            decay = mem["decay"][:, cols]
+            rates_now = [delta[at, cols] for at in ats]
+            push_now = [push[at, cols] for at in ats]
+            read = [[] for _ in ats]
+            for u in range(8):
+                r = block * 8 + u
+                hidden = mem["state"][r, :, cols].astype(jnp.float32)
+                for s in range(steps):
+                    gain_in = gains[s * requests + r, :state_width]
+                    gain_out = gains[s * requests + r, state_width:]
+                    gain_in = jnp.concatenate([gain_in, gain_in], axis=1)
+                    gain_out = jnp.concatenate([gain_out, gain_out], axis=1)
+                    hidden = (
+                        jnp.exp(-rates_now[s][u : u + 1] * decay) * hidden
+                        + push_now[s][u : u + 1] * gain_in
+                    )
+                    read[s].append(jnp.sum(hidden * gain_out, axis=0, keepdims=True))
+                final = hidden.astype(states[half].dtype)
+                states[half][2 * b, r] = final[:, :HEAD]
+                states[half][2 * b + 1, r] = final[:, HEAD:]
+            for s in range(steps):
+                reading[ats[s], cols] = jnp.concatenate(read[s])
+
+    def gate():
+        load("gate").wait()
+        load("skip").wait()
+
+        @pl.loop(0, channels // 256)
+        def _(b):
+            cols = pl.ds(pl.multiple_of(b * 256, 256), 256)
+            for s in range(steps):
+                rows = slice(s * requests, (s + 1) * requests)
+                read = reading[rows, cols] + mem["skip"][:, cols] * conv_out[rows, cols].astype(jnp.float32)
+                mamba[s, :, cols] = (read * silu(mem["gate"][s, :, cols].astype(jnp.float32))).astype(mamba.dtype)
+
+        pltpu.make_async_copy(mamba, out_mamba, o_sem.at[0]).start()
+
+    group = mem["query"].shape[2] // HEAD // 2
+
+    def attend(half, g):
+        rows16 = slice(half * 16, half * 16 + 16)
+        query = jnp.concatenate(
+            [
+                mem["query"][s, rows16, (g * group + h) * HEAD : (g * group + h + 1) * HEAD]
+                for s in range(steps)
+                for h in range(group)
+            ]
+        )
+        size = query.shape[0]
+        row = lax.broadcasted_iota(jnp.int32, (size, 256), 0)
+        col = lax.broadcasted_iota(jnp.int32, (size, 256), 1)
+        limit = mem["lengths"][half : half + 1, :] + row // (size // steps)
+        scores = []
+        for p in range(2):
+            keys = caches[g * 2 + p, rows16].reshape(256, HEAD)
+            score = lax.dot_general(query, keys, nt, preferred_element_type=jnp.float32) / math.sqrt(HEAD)
+            allowed = (row % 16 == col // 16) & (col % 16 + p * 16 <= limit)
+            scores.append(jnp.where(allowed, score, -1e30))
+        highest = jnp.maximum(
+            jnp.max(scores[0], axis=-1, keepdims=True), jnp.max(scores[1], axis=-1, keepdims=True)
+        )
+        weights = [jnp.exp(score - highest) for score in scores]
+        whole = jnp.sum(weights[0], axis=-1, keepdims=True) + jnp.sum(weights[1], axis=-1, keepdims=True)
+        inverse = 1.0 / whole
+        mixed = jnp.zeros((size, HEAD), jnp.float32)
+        for p in range(2):
+            values = caches[4 + g * 2 + p, rows16].reshape(256, HEAD)
+            mixed = mixed + jnp.dot(
+                (weights[p] * inverse).astype(values.dtype), values, preferred_element_type=jnp.float32
+            )
+        mixed = mixed.astype(attn.dtype)
+        for s in range(steps):
+            for h in range(group):
+                at = (s * group + h) * 16
+                attn[s, rows16, (g * group + h) * HEAD : (g * group + h + 1) * HEAD] = mixed[at : at + 16]
+
+    begin(0)
+    update_caches()
+    begin(1)
+    convolve()
+    project()
+    pack(0)
+    load("query").wait()
+    load("lengths").wait()
+    for half in range(2):
+        attend(half, 0)
+    pack(1)
+    load("decay").wait()
+    load("state").wait()
+    rates()
+    recur(0)
+    begin(2)
+    forward(0, 1)
+    recur(1)
+    begin(3)
+    forward(1, 1)
+    forward(0, 2)
+    for half in range(2):
+        attend(half, 1)
+    pltpu.make_async_copy(attn, out_attn, o_sem.at[1]).start()
+    pack(2)
+    gate()
+    forward(1, 2)
+    forward(0, 3)
+    pack(3)
+    forward(2, 1)
+    forward(1, 3)
+    unpack(0)
+    forward(3, 1)
+    forward(2, 2)
+    unpack(1)
+    forward(3, 2)
+    forward(2, 3)
+    forward(3, 3)
+    unpack(2)
+    unpack(3)
+
     for k in range(count):
         for o in range(1, RANKS):
             gather_copy(k, o).wait_recv()
         gather_self(k).wait()
+    pltpu.make_async_copy(mamba, out_mamba, o_sem.at[0]).wait()
+    pltpu.make_async_copy(attn, out_attn, o_sem.at[1]).wait()
     for k in range(count):
         for o in range(1, RANKS):
             spread_copy(k, o).wait_send()
@@ -207,19 +509,45 @@
         for d in range(2):
             for h in range(4):
                 ring_copy(k, d, h).wait_send()
-
-
-def migrate(tables, parts):
-    count = len(parts)
-    width = RANKS * parts[0].shape[1]
+    for o in range(1, tensors):
+        for copy in share_copies(o):
+            copy.wait_send()
+
+
+def fast_steps(tables, kv_length, final_conv, loads, outs):
+    requests, _, channels = final_conv.shape
+    steps = loads["query"].shape[0]
+    width = RANKS * requests
+    kind = final_conv.dtype
+    slices = [(final_conv.shape[1], 2 * HEAD), (16, HEAD), (16, HEAD), (16, HEAD)]
+    count = len(slices)
+    rank_width = loads["dtproj"].shape[0]
+    gains = loads["xproj"].shape[0] - rank_width
+    rows = steps * requests
+    tensors = lax.axis_size("tensor")
     smem = pl.BlockSpec(memory_space=pltpu.SMEM)
     anywhere = pl.BlockSpec(memory_space=pl.ANY)
-    scratch = []
+    f32 = jnp.float32
+    scratch = [pltpu.VMEM(loads[name].shape, loads[name].dtype) for name in LOADS]
     for slots in (width, 2 * CAPS[0], 2 * sum(CAPS), width):
-        for part in parts:
-            scratch.append(pltpu.VMEM((slots,) + part.shape[2:], part.dtype))
+        scratch += [pltpu.VMEM((slots,) + each, kind) for each in slices]
+    scratch += [pltpu.VMEM((RANKS, requests) + each, kind) for each in slices[1:]]
+    scratch += [
+        pltpu.VMEM(loads["key_new"].shape, f32),
+        pltpu.VMEM(loads["value_new"].shape, f32),
+        pltpu.VMEM((rows, channels), kind),
+        pltpu.VMEM((tensors, rows, rank_width), f32),
+        pltpu.VMEM((tensors, gains, HEAD), f32),
+        pltpu.VMEM((rows, channels), f32),
+        pltpu.VMEM((rows, channels), f32),
+        pltpu.VMEM((rows, channels), f32),
+        pltpu.VMEM((rows, gains, HEAD), f32),
+        pltpu.VMEM((steps, requests, channels), kind),
+        pltpu.VMEM((steps, requests, channels), kind),
+    ]
     dma = pltpu.SemaphoreType.DMA
     scratch += [
+        dma((len(LOADS),)),
         dma((count, RANKS)),
         dma((count, RANKS)),
         dma((count,)),
@@ -228,50 +556,26 @@
         dma((count, RANKS)),
         dma((count, RANKS)),
         dma((count,)),
+        dma((2, tensors)),
+        dma((2, tensors)),
+        dma((2,)),
     ]
     return pl.pallas_call(
-        functools.partial(migrate_kernel, count),
-        out_shape=[jax.ShapeDtypeStruct(part.shape, part.dtype) for part in parts],
-        in_specs=[smem] * 4 + [anywhere] * count,
-        out_specs=[anywhere] * count,
+        functools.partial(step_kernel, slices),
+        out_shape=[jax.ShapeDtypeStruct(shape, kind) for shape in outs],
+        in_specs=[smem, smem] + [anywhere] * (1 + len(LOADS)),
+        out_specs=[anywhere] * 6,
         scratch_shapes=scratch,
         compiler_params=pltpu.CompilerParams(
-            collective_id=0, has_side_effects=True, vmem_limit_bytes=48 * 2**20
+            collective_id=0, has_side_effects=True, vmem_limit_bytes=56 * 2**20
         ),
-    )(*tables, *parts)
-
-
-def cut(final_conv, final_state, key_rows, value_rows):
-    requests, taps, channels = final_conv.shape
-    states = final_state.shape[1]
-    positions, width = key_rows.shape[1:]
-
-    def cache(rows):
-        split = rows.reshape(requests, positions // 16, 16, width // HEAD, HEAD)
-        return split.transpose(3, 1, 0, 2, 4).reshape(-1, requests, 16, HEAD)
-
-    conv = final_conv.reshape(requests, taps, RANKS, -1, HEAD).transpose(2, 0, 1, 3, 4)
-    conv = conv.reshape(RANKS, requests, -1, HEAD)
-    conv = jnp.pad(conv, ((0, 0), (0, 0), (0, 8 - conv.shape[2]), (0, 0)))
-    state = final_state.reshape(requests, states, -1, RANKS, HEAD).transpose(2, 3, 0, 1, 4)
-    return [jnp.concatenate([cache(key_rows), cache(value_rows)]), conv] + list(state)
-
-
-def join(parts, shapes):
-    caches, conv, *state = parts
-    requests, taps, channels = shapes[0]
-    positions, width = shapes[2][1:]
-
-    def cache(rows):
-        split = rows.reshape(width // HEAD, positions // 16, requests, 16, HEAD)
-        return split.transpose(2, 1, 3, 0, 4).reshape(requests, positions, width)
-
-    half = caches.shape[0] // 2
-    pieces = channels // (RANKS * HEAD)
-    conv = conv[:, :, : taps * pieces].reshape(RANKS, requests, taps, pieces, HEAD)
-    conv = conv.transpose(1, 2, 0, 3, 4).reshape(shapes[0])
-    state = jnp.stack(state).transpose(2, 3, 0, 1, 4).reshape(shapes[1])
-    return conv, state, cache(caches[:half]), cache(caches[half:])
+    )(tables, kv_length, final_conv, *[loads[name] for name in LOADS])
+
+
+def project_rows(conv_rows, xproj_weight):
+    return lax.dot_general(
+        conv_rows, xproj_weight, (((1,), (1,)), ((), ())), preferred_element_type=jnp.float32
+    )
 
 
 def slot_ranks(owners):
@@ -325,7 +629,7 @@
     )
 
 
-def local(
+def plain_steps(
     inner_input,
     gate_input,
     conv_state,
@@ -417,13 +721,87 @@
         )
         attended.append(mixed_out.reshape(requests_here, query_heads * HEAD).astype(jnp.bfloat16))
     arrays = (final_conv, final_state, key_rows, value_rows)
-    fits, *tables = route_tables(new_owner, lax.axis_index("section") // RANKS)
-    moved = lax.cond(
-        fits,
-        lambda: join(migrate(tables, cut(*arrays)), [a.shape for a in arrays]),
-        lambda: exchange(new_owner, arrays),
-    )
+    moved = exchange(new_owner, arrays)
     return (jnp.stack(mamba_list), jnp.stack(attended), *moved)
+
+
+def local(
+    inner_input,
+    gate_input,
+    conv_state,
+    mamba_state,
+    conv_weight,
+    conv_bias,
+    xproj_weight,
+    dt_gain,
+    dtproj_weight,
+    dt_bias,
+    decay_rate,
+    skip_gain,
+    query,
+    key_cache,
+    value_cache,
+    key_new,
+    value_new,
+    kv_length,
+    new_owner,
+):
+    steps, requests, channels = inner_input.shape
+    positions, width = key_cache.shape[1:]
+    tables = route_tables(new_owner)
+    final_conv = jnp.concatenate([conv_state[:, steps:], jnp.swapaxes(inner_input, 0, 1)], axis=1)
+    loads = {
+        "key_cache": key_cache,
+        "value_cache": value_cache,
+        "key_new": key_new.reshape(steps * requests, width),
+        "value_new": value_new.reshape(steps * requests, width),
+        "window": jnp.concatenate([jnp.swapaxes(conv_state, 0, 1), inner_input]),
+        "conv_weight": conv_weight,
+        "conv_bias": conv_bias.reshape(1, channels),
+        "xproj": xproj_weight,
+        "query": query,
+        "lengths": jnp.repeat(kv_length.reshape(2, requests // 2), 16, axis=1),
+        "dt_gain": dt_gain.reshape(1, -1),
+        "dtproj": dtproj_weight,
+        "dt_bias": dt_bias.reshape(1, channels),
+        "decay": decay_rate,
+        "state": mamba_state,
+        "gate": gate_input,
+        "skip": skip_gain.reshape(1, channels),
+    }
+    outs = [
+        inner_input.shape,
+        query.shape,
+        conv_state.shape,
+        mamba_state.shape,
+        key_cache.shape,
+        value_cache.shape,
+    ]
+    return lax.cond(
+        tables[4, 0] == 1,
+        lambda: tuple(fast_steps(tables, kv_length, final_conv, loads, outs)),
+        lambda: plain_steps(
+            inner_input,
+            gate_input,
+            conv_state,
+            mamba_state,
+            conv_weight,
+            conv_bias,
+            xproj_weight,
+            dt_gain,
+            dtproj_weight,
+            dt_bias,
+            decay_rate,
+            skip_gain,
+            query,
+            key_cache,
+            value_cache,
+            key_new,
+            value_new,
+            kv_length,
+            new_owner,
+        ),
+    )
 
 
 def solution(mesh):

time: 253 us -> 184 us (0.73)
  local copies, waits for them, and re-layouts: 50.9 us -> 14 us
  other arithmetic: 29.7 us -> 2.47 us
  Pallas kernels: 140 us -> 152 us
  matrix products: 9.84 us -> 0 us
  between operations: 19.7 us -> 14.7 us
    reduce_sum x6 -> x0, other arithmetic: 11.9 us -> none  [the longest x1 6.06 us: local(): jnp.sum(hidden * output_gain[:, :, None], axis=1) + skip_gain * inputs_now]
    pallas_call x1 -> x2, Pallas kernels: 140 us -> 152 us  [the longest x1 150 us: fast_steps(): pl.pallas_call(functools.partial(step_kernel, slices), out_shape=[jax.Sha...]
    dot_general x8 -> x0, matrix products: 9.84 us -> none  [the longest x2 3.99 us: local(): jnp.einsum('rgqc,rcgd->rgqd', weights, value_heads, preferred_element_typ...]
    reshape x13 -> x3, local copies, waits for them, and re-layouts: 10.3 us -> 2.7 us  [the longest x1 1.3 us: route_tables(): new_owner.reshape(PLANES, width)]
    sub x6 -> x0, local copies, waits for them, and re-layouts: 7.09 us -> none  [the longest x2 2.62 us: route_tables(): rank - ties + ties_up]
    transpose x5 -> x0, local copies, waits for them, and re-layouts: 6.02 us -> none  [the longest x1 3.78 us: join(): state = jnp.stack(state).transpose(2, 3, 0, 1, 4).reshape(shapes[1])]
    select_n x3 -> x0, other arithmetic: 4.84 us -> none  [the longest x1 2.66 us: route_tables(): lane = jnp.where((my_up == 1) & (my_place >= CAPS[0]), -1, lane)]
    unnamed x77 -> x9, local copies, waits for them, and re-layouts: 3.27 us -> 7.84 us
  transfers between devices with their start and end apart: 1 -> 0, of which waited for: 1 -> 0; matrix products, arithmetic and copies ran while one was open for 16% -> 0% of each run, Pallas kernels for 0% -> 0%
where the time goes in v2:
time: 184 us; the launch traced here: 183 us
  Pallas kernels  152 us (83%)
  between operations  14.7 us (8%)
  local copies, waits for them, and re-layouts  14 us (8%)
  other arithmetic  2.47 us (1%)
    pallas_call x1, Pallas kernels, fast_steps(): pl.pallas_call(functools.partial(step_kernel, slices), out_shape=[jax.Sha...  150 us
    unnamed x9, local copies, waits for them, and re-layouts  7.84 us

profile of v2, /device:TPU:1, one launch (start us, length us, event | category | flops | bytes accessed | tf_op | source)
XLA Modules:
  0.0 183.2 jit_solution(7916214529409055302)
XLA Ops:
  7.2 1.3 reshape.731.owner_ref
  8.5 1.5 shard_map.238
  10.0 0.9 slice.86
  10.9 0.2 copy.65
  11.2 1.2 copy.99
  12.4 1.3 pad_maximum_fusion.4
  13.7 1.1 pad_maximum_fusion.3
  14.9 0.5 slice.95
  16.0 153.9 %conditional.1 = (bf16[2,32,2048]{2,1,0:T(8,128)(2,1)S(1)}, bf16[2,32,2048]{2,1,0:T(8,128)(2,1)}, bf16[32,16,2048]{2,1,0:T(8,128)(2,1)S(1)}, bf16[32,32,256]{2,1...) conditional(s32[]{:T(128)} %bitcast.33, (f32[2048]{0:T(1024)}, ...), branch_computations={%region_0.18_spmd, %region_18.19_spmd} | conditional | flops 545451264 | bytes 145830096 | solution.py:780
  16.3 0.0 copy-start.29
  16.3 0.6 copy-done.29
  16.9 0.7 reshape.725
  17.6 0.1 broadcast_in_dim.145
  17.7 0.7 reshape.726.refs_9_
  18.3 150.3 %branch_1_fun.1 = (bf16[2,32,2048]{2,1,0:T(8,128)(2,1)S(1)}, bf16[2,32,2048]{2,1,0:T(8,128)(2,1)}, bf16[32,3,2048]{2,1,0:T(4,128)(2,1)}, bf16[32,16,2048]{2,1,0:...) custom-call(s32[8,256]{1,0:T(8,128)} %copy-done.29, s32[32]{0:T(128)} %get-tuple-element.106.kv_len, ...), custom_call_target="tpu_custom_call" | custom-call | tf_op jit(solution)/shard_map/cond/branch_1_fun/pallas_call | solution.py:563
  168.6 1.3 copy.64
  170.0 0.0 copy-start.16
  170.0 0.8 copy.123
  170.7 1.7 copy.124
  172.4 1.3 copy.125
  173.7 0.8 copy.126
  174.5 1.9 %copy.127 = bf16[32,32,256]{2,1,0:T(8,128)(2,1)} copy(bf16[32,32,256]{2,1,0:T(8,128)(2,1)} %get-tuple-element.233) | data formatting | bytes 1048576
  176.4 0.0 copy-done.16
Async XLA Ops:
  16.3 0.6 copy-start.29
  170.0 6.4 %copy-start.16 = (bf16[32,3,2048]{2,0,1:T(8,128)(2,1)}, bf16[32,3,2048]{2,0,1:T(8,128)(2,1)S(1)}, u32[]{:S(2)}) copy-start(bf16[32,3,2048]{2,0,1:T(8,128)(2,1)S(1)} %get-tuple-element.230) | copy-start | bytes 1179652
